TPU v7x, 32 devices: a whole 2x2x4 slice. The times are simulated.
32 devices in a mesh: dp: 16 (over z, y, core), fsdp: 2 (over x).
Axes of the slice: x: 2, y: 2, z: 4, core: 2. Of those that a mesh axis runs over, the one named last changes fastest.
Arguments:
- tokens: bfloat16 [16384, 1024], P(('dp', 'fsdp')), may hold values from -6 to 6
- lengths: int32 [64], P(('dp', 'fsdp')), may hold values from 32 to 256, as said below
- cotangent: bfloat16 [16384, 1024], P(('dp', 'fsdp')), may hold values from -6 to 6
- early_norm: bfloat16 [1024], P('fsdp'), may hold values from 0.25 to 1.75
- early_up: bfloat16 [1024, 4096], P(None, 'fsdp'), may hold values from -0.1875 to 0.1875
- early_down: bfloat16 [4096, 1024], P('fsdp'), may hold values from -0.09375 to 0.09375
- attend_norm: bfloat16 [1024], P('fsdp'), may hold values from 0.25 to 1.75
- heads_weight: bfloat16 [1024, 3072], P('fsdp'), may hold values from -0.1875 to 0.1875
- position_weight: bfloat16 [1024, 1024], P('fsdp'), may hold values from -0.1875 to 0.1875
- content_bias: bfloat16 [1024], P('fsdp'), may hold values from -3 to 3
- position_bias: bfloat16 [1024], P('fsdp'), may hold values from -3 to 3
- attend_output: bfloat16 [1024, 1024], P('fsdp'), may hold values from -0.75 to 0.75
- mixer_norm: bfloat16 [1024], P('fsdp'), may hold values from 0.25 to 1.75
- gating_weight: bfloat16 [1024, 2048], P('fsdp'), may hold values from -0.1875 to 0.1875
- depth_kernel: bfloat16 [5, 1024], P(None, 'fsdp'), may hold values from -2.5 to 2.5
- batch_gain: bfloat16 [1024], P('fsdp'), may hold values from 0.25 to 1.75
- batch_shift: bfloat16 [1024], P('fsdp'), may hold values from -3 to 3
- mixer_output: bfloat16 [1024, 1024], P('fsdp'), may hold values from -0.1875 to 0.1875
- late_norm: bfloat16 [1024], P('fsdp'), may hold values from 0.25 to 1.75
- late_up: bfloat16 [1024, 4096], P(None, 'fsdp'), may hold values from -0.1875 to 0.1875
- late_down: bfloat16 [4096, 1024], P('fsdp'), may hold values from -0.09375 to 0.09375
- final_gain: bfloat16 [1024], P('fsdp'), may hold values from 0.25 to 1.75
Outputs:
- out: bfloat16 [16384, 1024], P(('dp', 'fsdp'))
- grad_tokens: bfloat16 [16384, 1024], P(('dp', 'fsdp'))
- grad_early_norm: float32 [1024], P('fsdp')
- grad_early_up: float32 [1024, 4096], P(None, 'fsdp')
- grad_early_down: float32 [4096, 1024], P('fsdp')
- grad_attend_norm: float32 [1024], P('fsdp')
- grad_heads_weight: float32 [1024, 3072], P('fsdp')
- grad_position_weight: float32 [1024, 1024], P('fsdp')
- grad_content_bias: float32 [1024], P('fsdp')
- grad_position_bias: float32 [1024], P('fsdp')
- grad_attend_output: float32 [1024, 1024], P('fsdp')
- grad_mixer_norm: float32 [1024], P('fsdp')
- grad_gating_weight: float32 [1024, 2048], P('fsdp')
- grad_depth_kernel: float32 [5, 1024], P(None, 'fsdp')
- grad_batch_gain: float32 [1024], P('fsdp')
- grad_batch_shift: float32 [1024], P('fsdp')
- grad_mixer_output: float32 [1024, 1024], P('fsdp')
- grad_late_norm: float32 [1024], P('fsdp')
- grad_late_up: float32 [1024, 4096], P(None, 'fsdp')
- grad_late_down: float32 [4096, 1024], P('fsdp')
- grad_final_gain: float32 [1024], P('fsdp')
Inputs may be any that keep to these rules, and one draw needn't show every extreme that they name: Utterance i fills the first lengths[i] frames of its slot; in every draw some utterance fills all 256 frames.
All inputs are finite; a program needn't handle non-finite values.
Results may differ from a plain program's by a relative error of at most 0.025.
Values may be sent and summed in bfloat16 or wider, within the bound.
No kernel may reach another device: no remote copies, remote signals or barrier semaphores. Data moves between devices by JAX's collectives and lax.ppermute only.
A program may use at most 320 MiB of HBM per device.

v0:
```python
import math

import jax
import jax.numpy as jnp
from jax import lax
from jax.sharding import PartitionSpec as P

HEAD_DIM = 128


def layer_norm(signal, norm_gain):
    average = jnp.mean(signal, axis=-1, keepdims=True)
    centred = signal - average
    spread = jnp.mean(centred * centred, axis=-1, keepdims=True)
    return centred * lax.rsqrt(spread + 1e-05) * norm_gain


def gated_units(joined):
    half_width = joined.shape[-1] // 2
    return joined[:, :half_width] * jax.nn.sigmoid(joined[:, half_width:])


def depthwise(signal, kernel):
    kernel_taps = kernel.shape[0]
    left_pad = (kernel_taps - 1) // 2
    frames = signal.shape[0]
    padded = jnp.pad(signal, ((left_pad, kernel_taps - 1 - left_pad), (0, 0)))
    running = jnp.zeros_like(signal)
    for offset in range(kernel_taps):
        running = running + padded[offset : offset + frames] * kernel[offset]
    return running


def slot_conv(signal, kernel, frames):
    model_width = signal.shape[1]
    pieces = signal.reshape(-1, frames, model_width)
    return jax.vmap(depthwise, (0, None))(pieces, kernel).reshape(signal.shape)


def batch_moments(first, second, frames_total):
    average = first / frames_total
    spread = second / frames_total - average * average
    return (average, lax.rsqrt(spread + 1e-05))


def batch_apply(mixed, average, inv_scale, scale_gain, shift_bias):
    return (mixed - average) * inv_scale * scale_gain + shift_bias


def rel_shift(spanning):
    head_count, frames, span_width = spanning.shape
    flat = spanning.reshape(head_count, frames * span_width)
    flat = flat[:, frames - 1 : frames - 1 + frames * (span_width - 1)]
    return flat.reshape(head_count, frames, span_width - 1)[:, :, :frames]


def sinusoid(frames, model_width):
    distance = (frames - 1 - jnp.arange(2 * frames - 1)).astype(jnp.float32)
    halves = model_width // 2
    frequency = jnp.exp(
        jnp.arange(halves).astype(jnp.float32) * (-2.0 * math.log(10000.0) / model_width)
    )
    angles = distance[:, None] * frequency[None, :]
    return jnp.concatenate([jnp.sin(angles), jnp.cos(angles)], axis=1)


def product(form, left, right):
    return jnp.einsum(form, left, right, preferred_element_type=jnp.float32)


def prepare_ffn(norm_gain, up_weight, down_weight):
    return (
        lax.all_gather(norm_gain, "fsdp", axis=0, tiled=True),
        lax.all_gather(up_weight, "fsdp", axis=1, tiled=True),
        lax.all_gather(down_weight, "fsdp", axis=0, tiled=True),
    )


def gather_attend(
    norm_gain, heads_weight, position_weight, content_bias, position_bias, output_weight, final_gain
):
    return (
        lax.all_gather(norm_gain, "fsdp", axis=0, tiled=True),
        lax.all_gather(heads_weight, "fsdp", axis=0, tiled=True),
        lax.all_gather(position_weight, "fsdp", axis=0, tiled=True),
        lax.all_gather(content_bias, "fsdp", axis=0, tiled=True),
        lax.all_gather(position_bias, "fsdp", axis=0, tiled=True),
        lax.all_gather(output_weight, "fsdp", axis=0, tiled=True),
        lax.all_gather(final_gain, "fsdp", axis=0, tiled=True),
    )


def gather_mixer(norm_gain, gating_weight, depth_kernel, batch_gain, batch_shift, output_weight):
    return (
        lax.all_gather(norm_gain, "fsdp", axis=0, tiled=True),
        lax.all_gather(gating_weight, "fsdp", axis=0, tiled=True),
        lax.all_gather(depth_kernel, "fsdp", axis=1, tiled=True),
        lax.all_gather(batch_gain, "fsdp", axis=0, tiled=True),
        lax.all_gather(batch_shift, "fsdp", axis=0, tiled=True),
        lax.all_gather(output_weight, "fsdp", axis=0, tiled=True),
    )


def ffn_forward(signal, weights):
    norm_gain, up_weight, down_weight = weights
    normed = layer_norm(signal, norm_gain.astype(jnp.float32)).astype(jnp.bfloat16)
    hidden = product("td,df->tf", normed, up_weight)
    active = jax.nn.silu(hidden).astype(jnp.bfloat16)
    return signal + 0.5 * product("tf,fd->td", active, down_weight)


def ffn_backward(signal, weights, upstream):
    norm_gain, up_weight, down_weight = weights
    normed_full, norm_pull = jax.vjp(layer_norm, signal, norm_gain.astype(jnp.float32))
    normed = normed_full.astype(jnp.bfloat16)
    out_grad = (0.5 * upstream).astype(jnp.bfloat16)
    hidden = product("td,df->tf", normed, up_weight)
    active_full, silu_pull = jax.vjp(jax.nn.silu, hidden)
    active = active_full.astype(jnp.bfloat16)
    grad_down = product("tf,td->fd", active, out_grad)
    grad_active = product("td,fd->tf", out_grad, down_weight)
    grad_hidden = silu_pull(grad_active)[0].astype(jnp.bfloat16)
    grad_up = product("td,tf->df", normed, grad_hidden)
    grad_normed = product("tf,df->td", grad_hidden, up_weight)
    grad_signal, grad_gain = norm_pull(grad_normed)
    shards = (
        lax.psum_scatter(
            grad_gain.astype(jnp.bfloat16), "fsdp", scatter_dimension=0, tiled=True
        ).astype(jnp.float32),
        lax.psum_scatter(
            grad_up.astype(jnp.bfloat16), "fsdp", scatter_dimension=1, tiled=True
        ).astype(jnp.float32),
        lax.psum_scatter(
            grad_down.astype(jnp.bfloat16), "fsdp", scatter_dimension=0, tiled=True
        ).astype(jnp.float32),
    )
    return (upstream + grad_signal, shards)


def attend_block(signal, weights, key_valid, table, upstream):
    (
        norm_gain,
        heads_weight,
        position_weight,
        content_bias,
        position_bias,
        output_weight,
        final_gain,
    ) = weights
    utterances, frames = key_valid.shape
    rows_total, model_width = signal.shape
    head_count = model_width // HEAD_DIM
    head_shape = (utterances, frames, head_count, HEAD_DIM)
    score_scale = 1.0 / math.sqrt(HEAD_DIM)
    normed_full, norm_pull = jax.vjp(layer_norm, signal, norm_gain.astype(jnp.float32))
    normed = normed_full.astype(jnp.bfloat16)
    joined = product("td,de->te", normed, heads_weight)
    queries = joined[:, :model_width]
    key_rows = joined[:, model_width : 2 * model_width].astype(jnp.bfloat16).reshape(head_shape)
    value_rows = joined[:, 2 * model_width :].astype(jnp.bfloat16).reshape(head_shape)
    q_content = (
        (queries + content_bias.astype(jnp.float32)).astype(jnp.bfloat16).reshape(head_shape)
    )
    q_position = (
        (queries + position_bias.astype(jnp.float32)).astype(jnp.bfloat16).reshape(head_shape)
    )
    relative = product("nc,cd->nd", table, position_weight).astype(jnp.bfloat16)
    relative = relative.reshape(2 * frames - 1, head_count, HEAD_DIM)
    content = product("uihd,ujhd->uhij", q_content, key_rows)
    shifted, shift_pull = jax.vjp(
        jax.vmap(rel_shift), product("uihd,nhd->uhin", q_position, relative)
    )
    scores = jnp.where(key_valid[:, None, None, :], (content + shifted) * score_scale, -1e30)
    weighting = jax.nn.softmax(scores, axis=-1)
    weighting_low = weighting.astype(jnp.bfloat16)
    context = product("uhij,ujhd->uihd", weighting_low, value_rows).reshape(rows_total, model_width)
    context = context.astype(jnp.bfloat16)
    if upstream is None:
        return signal + product("td,de->te", context, output_weight)
    out_grad = upstream.astype(jnp.bfloat16)
    grad_output = product("td,te->de", context, out_grad)
    grad_context = (
        product("te,de->td", out_grad, output_weight).astype(jnp.bfloat16).reshape(head_shape)
    )
    grad_weighting = product("uihd,ujhd->uhij", grad_context, value_rows)
    grad_values = product("uhij,uihd->ujhd", weighting_low, grad_context)
    grad_scores = weighting * (
        grad_weighting - jnp.sum(grad_weighting * weighting, axis=-1, keepdims=True)
    )
    grad_raw = (grad_scores * score_scale).astype(jnp.bfloat16)
    grad_q_content = product("uhij,ujhd->uihd", grad_raw, key_rows)
    grad_keys = product("uhij,uihd->ujhd", grad_raw, q_content)
    grad_spanning = shift_pull(grad_raw.astype(jnp.float32))[0].astype(jnp.bfloat16)
    grad_q_position = product("uhin,nhd->uihd", grad_spanning, relative)
    grad_relative = product("uhin,uihd->nhd", grad_spanning, q_position)
    grad_relative = grad_relative.reshape(2 * frames - 1, model_width).astype(jnp.bfloat16)
    grad_position = product("nc,nd->cd", table, grad_relative)
    grad_content_bias = jnp.sum(grad_q_content, axis=(0, 1)).reshape(model_width)
    grad_position_bias = jnp.sum(grad_q_position, axis=(0, 1)).reshape(model_width)
    grad_joined = jnp.concatenate(
        [
            (grad_q_content + grad_q_position).reshape(rows_total, model_width),
            grad_keys.reshape(rows_total, model_width),
            grad_values.reshape(rows_total, model_width),
        ],
        axis=1,
    ).astype(jnp.bfloat16)
    grad_heads = product("td,te->de", normed, grad_joined)
    grad_normed = product("te,de->td", grad_joined, heads_weight)
    grad_signal, grad_gain = norm_pull(grad_normed)
    return (
        upstream + grad_signal,
        (grad_gain, grad_heads, grad_position, grad_content_bias, grad_position_bias, grad_output),
    )


def mixer_block(signal, weights, frame_mask, frames, totals, upstream):
    norm_gain, gating_weight, depth_kernel, batch_gain, batch_shift, output_weight = weights
    normed_full, norm_pull = jax.vjp(layer_norm, signal, norm_gain.astype(jnp.float32))
    normed = normed_full.astype(jnp.bfloat16)
    joined = product("td,de->te", normed, gating_weight)
    gated, gate_pull = jax.vjp(gated_units, joined)
    mixed, conv_pull = jax.vjp(
        lambda values, taps: slot_conv(values, taps, frames),
        gated * frame_mask,
        depth_kernel.astype(jnp.float32),
    )
    if totals is None:
        totals = lax.psum(
            (
                jnp.sum(frame_mask * mixed, axis=0),
                jnp.sum(frame_mask * mixed * mixed, axis=0),
                jnp.sum(frame_mask),
            ),
            ("dp", "fsdp"),
        )
    first, second, frames_total = totals
    moments, moment_pull = jax.vjp(
        lambda summed_first, summed_second: batch_moments(
            summed_first, summed_second, frames_total
        ),
        first,
        second,
    )
    bn_out, apply_pull = jax.vjp(
        batch_apply,
        mixed,
        moments[0],
        moments[1],
        batch_gain.astype(jnp.float32),
        batch_shift.astype(jnp.float32),
    )
    active_full, silu_pull = jax.vjp(jax.nn.silu, bn_out)
    active = active_full.astype(jnp.bfloat16)
    if upstream is None:
        return (signal + product("td,de->te", active, output_weight), totals)
    out_grad = upstream.astype(jnp.bfloat16)
    grad_output = product("td,te->de", active, out_grad)
    grad_active = product("te,de->td", out_grad, output_weight)
    grad_bn = silu_pull(grad_active)[0]
    grad_mixed, grad_average, grad_inverse, grad_scale, grad_shift = apply_pull(grad_bn)
    grad_average, grad_inverse = lax.psum((grad_average, grad_inverse), ("dp", "fsdp"))
    grad_first, grad_second = moment_pull((grad_average, grad_inverse))
    grad_mixed = grad_mixed + frame_mask * (grad_first + 2.0 * mixed * grad_second)
    grad_gated, grad_kernel = conv_pull(grad_mixed)
    grad_joined = gate_pull(grad_gated * frame_mask)[0].astype(jnp.bfloat16)
    grad_gating = product("td,te->de", normed, grad_joined)
    grad_normed = product("te,de->td", grad_joined, gating_weight)
    grad_signal, grad_gain = norm_pull(grad_normed)
    return (
        upstream + grad_signal,
        (grad_gain, grad_gating, grad_kernel, grad_scale, grad_shift, grad_output),
    )


def on_device(
    tokens,
    lengths,
    cotangent,
    early_norm,
    early_up,
    early_down,
    attend_norm,
    heads_weight,
    position_weight,
    content_bias,
    position_bias,
    attend_output,
    mixer_norm,
    gating_weight,
    depth_kernel,
    batch_gain,
    batch_shift,
    mixer_output,
    late_norm,
    late_up,
    late_down,
    final_gain,
):
    utterances = lengths.shape[0]
    frames = tokens.shape[0] // utterances
    key_valid = lax.iota(jnp.int32, frames)[None, :] < lengths[:, None]
    frame_mask = key_valid.reshape(-1, 1).astype(jnp.float32)
    table = sinusoid(frames, tokens.shape[1]).astype(jnp.bfloat16)
    start = tokens.astype(jnp.float32)
    early = prepare_ffn(early_norm, early_up, early_down)
    after_early = ffn_forward(start, early)
    attend = gather_attend(
        attend_norm,
        heads_weight,
        position_weight,
        content_bias,
        position_bias,
        attend_output,
        final_gain,
    )
    after_attend = attend_block(after_early, attend, key_valid, table, None)
    mixer = gather_mixer(
        mixer_norm, gating_weight, depth_kernel, batch_gain, batch_shift, mixer_output
    )
    after_mixer, totals = mixer_block(after_attend, mixer, frame_mask, frames, None, None)
    late = prepare_ffn(late_norm, late_up, late_down)
    after_late = ffn_forward(after_mixer, late)
    output, final_pull = jax.vjp(layer_norm, after_late, attend[6].astype(jnp.float32))
    upstream, grad_final = final_pull(cotangent.astype(jnp.float32) * frame_mask)
    late_back = prepare_ffn(late_norm, late_up, late_down)
    upstream, late_shards = ffn_backward(after_mixer, late_back, upstream)
    mixer_back = gather_mixer(
        mixer_norm, gating_weight, depth_kernel, batch_gain, batch_shift, mixer_output
    )
    upstream, mixer_grads = mixer_block(
        after_attend, mixer_back, frame_mask, frames, totals, upstream
    )
    attend_back = gather_attend(
        attend_norm,
        heads_weight,
        position_weight,
        content_bias,
        position_bias,
        attend_output,
        final_gain,
    )
    upstream, attend_grads = attend_block(after_early, attend_back, key_valid, table, upstream)
    middle = (
        lax.psum_scatter(
            attend_grads[0].astype(jnp.bfloat16), "fsdp", scatter_dimension=0, tiled=True
        ).astype(jnp.float32),
        lax.psum_scatter(
            attend_grads[1].astype(jnp.bfloat16), "fsdp", scatter_dimension=0, tiled=True
        ).astype(jnp.float32),
        lax.psum_scatter(
            attend_grads[2].astype(jnp.bfloat16), "fsdp", scatter_dimension=0, tiled=True
        ).astype(jnp.float32),
        lax.psum_scatter(
            attend_grads[3].astype(jnp.bfloat16), "fsdp", scatter_dimension=0, tiled=True
        ).astype(jnp.float32),
        lax.psum_scatter(
            attend_grads[4].astype(jnp.bfloat16), "fsdp", scatter_dimension=0, tiled=True
        ).astype(jnp.float32),
        lax.psum_scatter(
            attend_grads[5].astype(jnp.bfloat16), "fsdp", scatter_dimension=0, tiled=True
        ).astype(jnp.float32),
        lax.psum_scatter(
            mixer_grads[0].astype(jnp.bfloat16), "fsdp", scatter_dimension=0, tiled=True
        ).astype(jnp.float32),
        lax.psum_scatter(
            mixer_grads[1].astype(jnp.bfloat16), "fsdp", scatter_dimension=0, tiled=True
        ).astype(jnp.float32),
        lax.psum_scatter(
            mixer_grads[2].astype(jnp.bfloat16), "fsdp", scatter_dimension=1, tiled=True
        ).astype(jnp.float32),
        lax.psum_scatter(
            mixer_grads[3].astype(jnp.bfloat16), "fsdp", scatter_dimension=0, tiled=True
        ).astype(jnp.float32),
        lax.psum_scatter(
            mixer_grads[4].astype(jnp.bfloat16), "fsdp", scatter_dimension=0, tiled=True
        ).astype(jnp.float32),
        lax.psum_scatter(
            mixer_grads[5].astype(jnp.bfloat16), "fsdp", scatter_dimension=0, tiled=True
        ).astype(jnp.float32),
        lax.psum_scatter(
            grad_final.astype(jnp.bfloat16), "fsdp", scatter_dimension=0, tiled=True
        ).astype(jnp.float32),
    )
    early_back = prepare_ffn(early_norm, early_up, early_down)
    upstream, early_shards = ffn_backward(start, early_back, upstream)
    summed = (
        lax.psum(early_shards[0].astype(jnp.bfloat16), "dp").astype(jnp.float32),
        lax.psum(early_shards[1].astype(jnp.bfloat16), "dp").astype(jnp.float32),
        lax.psum(early_shards[2].astype(jnp.bfloat16), "dp").astype(jnp.float32),
        lax.psum(middle[0].astype(jnp.bfloat16), "dp").astype(jnp.float32),
        lax.psum(middle[1].astype(jnp.bfloat16), "dp").astype(jnp.float32),
        lax.psum(middle[2].astype(jnp.bfloat16), "dp").astype(jnp.float32),
        lax.psum(middle[3].astype(jnp.bfloat16), "dp").astype(jnp.float32),
        lax.psum(middle[4].astype(jnp.bfloat16), "dp").astype(jnp.float32),
        lax.psum(middle[5].astype(jnp.bfloat16), "dp").astype(jnp.float32),
        lax.psum(middle[6].astype(jnp.bfloat16), "dp").astype(jnp.float32),
        lax.psum(middle[7].astype(jnp.bfloat16), "dp").astype(jnp.float32),
        lax.psum(middle[8].astype(jnp.bfloat16), "dp").astype(jnp.float32),
        lax.psum(middle[9].astype(jnp.bfloat16), "dp").astype(jnp.float32),
        lax.psum(middle[10].astype(jnp.bfloat16), "dp").astype(jnp.float32),
        lax.psum(middle[11].astype(jnp.bfloat16), "dp").astype(jnp.float32),
        lax.psum(late_shards[0].astype(jnp.bfloat16), "dp").astype(jnp.float32),
        lax.psum(late_shards[1].astype(jnp.bfloat16), "dp").astype(jnp.float32),
        lax.psum(late_shards[2].astype(jnp.bfloat16), "dp").astype(jnp.float32),
        lax.psum(middle[12].astype(jnp.bfloat16), "dp").astype(jnp.float32),
    )
    return (
        output.astype(jnp.bfloat16),
        upstream.astype(jnp.bfloat16),
        summed[0],
        summed[1],
        summed[2],
        summed[3],
        summed[4],
        summed[5],
        summed[6],
        summed[7],
        summed[8],
        summed[9],
        summed[10],
        summed[11],
        summed[12],
        summed[13],
        summed[14],
        summed[15],
        summed[16],
        summed[17],
        summed[18],
    )


def solution(mesh):
    in_specs = (
        P(("dp", "fsdp"), None),
        P(("dp", "fsdp")),
        P(("dp", "fsdp"), None),
        P("fsdp"),
        P(None, "fsdp"),
        P("fsdp", None),
        P("fsdp"),
        P("fsdp", None),
        P("fsdp", None),
        P("fsdp"),
        P("fsdp"),
        P("fsdp", None),
        P("fsdp"),
        P("fsdp", None),
        P(None, "fsdp"),
        P("fsdp"),
        P("fsdp"),
        P("fsdp", None),
        P("fsdp"),
        P(None, "fsdp"),
        P("fsdp", None),
        P("fsdp"),
    )
    out_specs = (
        P(("dp", "fsdp"), None),
        P(("dp", "fsdp"), None),
        P("fsdp"),
        P(None, "fsdp"),
        P("fsdp", None),
        P("fsdp"),
        P("fsdp", None),
        P("fsdp", None),
        P("fsdp"),
        P("fsdp"),
        P("fsdp", None),
        P("fsdp"),
        P("fsdp", None),
        P(None, "fsdp"),
        P("fsdp"),
        P("fsdp"),
        P("fsdp", None),
        P("fsdp"),
        P(None, "fsdp"),
        P("fsdp", None),
        P("fsdp"),
    )
    return jax.shard_map(
        on_device, mesh=mesh, in_specs=in_specs, out_specs=out_specs, check_vma=False
    )
```

profile of v0, /device:TPU:0, one launch (start us, length us, event | category | flops | bytes accessed | tf_op | source)
XLA Modules:
  0.0 1981.4 jit_solution(15256816140831465940)
XLA Ops:
  14.3 5.2 all-gather
  20.3 4.4 all-gather.1
  24.7 4.4 all-gather.2
  29.0 4.4 all-gather.3
  33.4 4.5 all_gather.86
  38.0 4.4 all-gather.4
  42.3 4.3 all-gather.6
  46.7 4.3 all-gather.5
  55.4 4.3 all-gather.8
  69.0 82.4 %all-gather.19.cloned.1.call-done = bf16[1024,4096]{1,0:T(8,128)(2,1)} async-done(((bf16[1024,2048]{1,0:T(8,128)(2,1)}), bf16[1024,4096]{1,0:T(8,128)(2,1)}) %all-gather.19.cloned.1.call-update) | async-done | bytes 8388624 | tf_op jit(solution)/shard_map/all_gather | solution.py:74
  151.4 10.5 fusion.93
  161.9 95.1 %all-gather.21.cloned.1.call-done = bf16[4096,1024]{1,0:T(8,128)(2,1)} async-done(((bf16[2048,1024]{1,0:T(8,128)(2,1)}), bf16[4096,1024]{1,0:T(8,128)(2,1)}) %all-gather.21.cloned.1.call-update) | async-done | bytes 8388624 | tf_op jit(solution)/shard_map/all_gather | solution.py:75
  257.0 9.6 fusion.106
  267.1 71.8 %all-gather.23.cloned.1.call-done = bf16[1024,3072]{1,0:T(8,128)(2,1)} async-done(((bf16[512,3072]{1,0:T(8,128)(2,1)}), bf16[1024,3072]{1,0:T(8,128)(2,1)}) %all-gather.23.cloned.1.call-update) | async-done | bytes 6291472 | tf_op jit(solution)/shard_map/all_gather | solution.py:84
  338.8 5.7 fusion.107
  352.1 5.9 convolution_bitcast_fusion
  357.9 8.7 copy.90
  366.6 8.9 reshape.373
  375.5 9.4 slice.88
  384.9 12.5 reshape.374
  397.4 4.6 slice.89
  402.0 5.3 copy.122
  420.4 5.6 fusion.39
  426.1 14.2 copy.94
  445.4 5.3 fusion.97
  454.1 40.1 %all-reduce.25 = (f32[1024]{0:T(1024)S(1)}, f32[]{:T(128)}, f32[1024]{0:T(1024)S(1)}) all-reduce(f32[1024]{0:T(1024)S(1)} %get-tuple-element.39, f32[]{:T(128)} %convert_reduce_fusion.1, f32[1024]{0:T(1024)S(1)} %get-tuple-element.38), channel_id=1, replica_groups=mesh['dp'=16,'fsdp'=2] {'dp','fsdp'}, use_global_device_ids=true, to_apply=%region_13.14 | all-reduce | flops 2049 | bytes 16392 | tf_op jit(solution)/shard_map/psum | solution.py:229
  501.2 71.9 %all-gather.33.cloned.1.call-done = bf16[1024,4096]{1,0:T(8,128)(2,1)} async-done(((bf16[1024,2048]{1,0:T(8,128)(2,1)}), bf16[1024,4096]{1,0:T(8,128)(2,1)}) %all-gather.33.cloned.1.call-update) | async-done | bytes 8388624 | tf_op jit(solution)/shard_map/all_gather | solution.py:74
  573.1 12.9 fusion.98
  586.0 92.6 %all-gather.35.cloned.1.call-done = bf16[4096,1024]{1,0:T(8,128)(2,1)} async-done(((bf16[2048,1024]{1,0:T(8,128)(2,1)}), bf16[4096,1024]{1,0:T(8,128)(2,1)}) %all-gather.35.cloned.1.call-update) | async-done | bytes 8388624 | tf_op jit(solution)/shard_map/all_gather | solution.py:75
  678.7 11.0 fusion.111
  694.3 13.9 fusion.4
  708.2 7.6 multiply_reduce_fusion.3
  718.1 4.4 multiply_reduce_fusion.4
  722.5 39.5 %all-reduce.24 = (f32[1024]{0:T(1024)S(1)}, f32[1024]{0:T(1024)S(1)}) all-reduce(f32[1024]{0:T(1024)S(1)} %get-tuple-element.22, f32[1024]{0:T(1024)S(1)} %neg.47), channel_id=1, replica_groups=mesh['dp'=16,'fsdp'=2] {'dp','fsdp'}, use_global_device_ids=true, to_apply=%region_25.26 | all-reduce | flops 2048 | bytes 16384 | tf_op jit(solution)/shard_map/psum | solution.py:262
  762.8 4.6 multiply_reduce_fusion.7
  796.2 8.8 reshape.380
  805.0 5.4 pad.64
  810.4 11.3 convert_element_type.385
  838.9 6.7 convolution_convert_fusion.5
  848.0 8.6 fusion.69
  856.6 4.5 bitcast_reduce_fusion
  862.3 8.3 fusion.41
  872.4 5.6 fusion.42
  883.6 5.7 convolution_convert_fusion.4
  889.5 6.9 multiply_reduce_fusion.11
  898.4 12.6 fusion.7
  913.0 7.3 convolution_convert_fusion.3
  920.4 10.9 convolution_convert_fusion.2
  932.9 9.2 convolution_convert_fusion.1
  943.7 11.3 convolution_convert_fusion
  960.3 25.2 %reduce-scatter.21.cloned.1.call-done = bf16[512,2048]{1,0:T(8,128)(2,1)} async-done(((bf16[1024,2048]{1,0:T(8,128)(2,1)}), bf16[512,2048]{1,0:T(8,128)(2,1)}) %reduce-scatter.21.cloned.1.call-update) | async-done | bytes 2097168 | tf_op jit(solution)/shard_map/reduce_scatter | solution.py:366
  985.5 79.8 %reduce-scatter.15.cloned.1.call-done = bf16[512,3072]{1,0:T(8,128)(2,1)} async-done(((bf16[1024,3072]{1,0:T(8,128)(2,1)}), bf16[512,3072]{1,0:T(8,128)(2,1)}) %reduce-scatter.15.cloned.1.call-update) | async-done | bytes 3145744 | tf_op jit(solution)/shard_map/reduce_scatter | solution.py:348
  1065.3 102.1 %reduce-scatter.11.cloned.1.call-done = bf16[1024,2048]{1,0:T(8,128)(2,1)} async-done(((bf16[1024,4096]{1,0:T(8,128)(2,1)}), bf16[1024,2048]{1,0:T(8,128)(2,1)}) %reduce-scatter.11.cloned.1.call-update) | async-done | bytes 4194320 | tf_op jit(solution)/shard_map/reduce_scatter | solution.py:130
  1167.4 102.0 %reduce-scatter.13.cloned.1.call-done = bf16[2048,1024]{1,0:T(8,128)(2,1)} async-done(((bf16[4096,1024]{1,0:T(8,128)(2,1)}), bf16[2048,1024]{1,0:T(8,128)(2,1)}) %reduce-scatter.13.cloned.1.call-update) | async-done | bytes 4194320 | tf_op jit(solution)/shard_map/reduce_scatter | solution.py:133
  1269.4 102.1 %reduce-scatter.27.cloned.1.call-done = bf16[1024,2048]{1,0:T(8,128)(2,1)} async-done(((bf16[1024,4096]{1,0:T(8,128)(2,1)}), bf16[1024,2048]{1,0:T(8,128)(2,1)}) %reduce-scatter.27.cloned.1.call-update) | async-done | bytes 4194320 | tf_op jit(solution)/shard_map/reduce_scatter | solution.py:130
  1371.5 101.5 %reduce-scatter.29.cloned.1.call-done = bf16[2048,1024]{1,0:T(8,128)(2,1)} async-done(((bf16[4096,1024]{1,0:T(8,128)(2,1)}), bf16[2048,1024]{1,0:T(8,128)(2,1)}) %reduce-scatter.29.cloned.1.call-update) | async-done | bytes 4194320 | tf_op jit(solution)/shard_map/reduce_scatter | solution.py:133
  1474.9 8.4 fusion.23
  1485.7 7.1 all-reduce.28
  1496.7 63.4 %all-reduce.26 = (bf16[512]{0:T(512)(128)(2,1)S(1)}, bf16[512]{0:T(512)(128)(2,1)S(1)}, bf16[512]{0:T(512)(128)(2,1)S(1)}, bf16[512]{0:T(512)(128)(2,1)S(1)}, bf...) all-reduce(bf16[512]{0:T(512)(128)(2,1)S(1)} %dynamic-slice.1, ...), channel_id=1, replica_groups=mesh['dp'=16,'fsdp'=2] {'dp'}, use_global_device_ids=true, to_apply=%region_35.36 | all-reduce | flops 7168 | bytes 28672 | tf_op jit(solution)/shard_map/psum | solution.py:388
  1565.9 376.2 %all-reduce.31.cloned.1.call-done = (bf16[1024,2048]{1,0:T(8,128)(2,1)}, bf16[2048,1024]{1,0:T(8,128)(2,1)}, bf16[512,3072]{1,0:T(8,128)(2,1)}, bf16[512,1024]{1...) async-done(((bf16[1024,2048]{1,0:T(8,128)(2,1)}, ...) | async-done | bytes 25165840 | tf_op jit(solution)/shard_map/psum | solution.py:389
  1942.1 6.8 convert_element_type.392
  1948.9 4.4 convert_element_type.394
  1965.2 4.4 convert_element_type.427
  1969.6 4.4 convert_element_type.429
  (394 shorter events, 159.4 us)
Async XLA Ops:
  7.2 56.7 %all-gather.25.cloned.1.call-start = ((), (), s32[]{:S(2)}) async-start(), calls=%async_computation.13 | async-start | bytes 3145728 | tf_op jit(solution)/shard_map/all_gather | solution.py:85
  7.9 143.5 %all-gather.19.cloned.1.call-start = ((), (), s32[]{:S(2)}) async-start(), calls=%async_computation.10 | async-start | bytes 12582912 | tf_op jit(solution)/shard_map/all_gather | solution.py:74
  8.7 248.4 %all-gather.21.cloned.1.call-start = ((), (), s32[]{:S(2)}) async-start(), calls=%async_computation.11 | async-start | bytes 12582912 | tf_op jit(solution)/shard_map/all_gather | solution.py:75
  9.4 329.4 %all-gather.23.cloned.1.call-start = ((), (), s32[]{:S(2)}) async-start(), calls=%async_computation.12 | async-start | bytes 9437184 | tf_op jit(solution)/shard_map/all_gather | solution.py:84
  10.0 430.3 %all-gather.27.cloned.1.call-start = ((), (), s32[]{:S(2)}) async-start(), calls=%async_computation.14 | async-start | bytes 3145728 | tf_op jit(solution)/shard_map/all_gather | solution.py:88
  10.6 434.8 %all-gather.29.cloned.1.call-start = ((), (), s32[]{:S(2)}) async-start(), calls=%async_computation.15 | async-start | bytes 6291456 | tf_op jit(solution)/shard_map/all_gather | solution.py:96
  11.2 484.4 %all-gather.31.cloned.1.call-start = ((), (), s32[]{:S(2)}) async-start(), calls=%async_computation.16 | async-start | bytes 3145728 | tf_op jit(solution)/shard_map/all_gather | solution.py:100
  11.9 561.2 %all-gather.33.cloned.1.call-start = ((), (), s32[]{:S(2)}) async-start(), calls=%async_computation.17 | async-start | bytes 12582912 | tf_op jit(solution)/shard_map/all_gather | solution.py:74
  12.7 6.9 copy-start.6
  12.7 666.0 %all-gather.35.cloned.1.call-start = ((), (), s32[]{:S(2)}) async-start(), calls=%async_computation.18 | async-start | bytes 12582912 | tf_op jit(solution)/shard_map/all_gather | solution.py:75
  13.4 6.8 copy-start.90
  13.4 11.2 copy-start.91
  13.4 15.6 copy-start.92
  13.4 20.0 %copy-start.83 = (bf16[5,512]{1,0:T(8,128)(2,1)S(1)}, bf16[5,512]{1,0:T(8,128)(2,1)}, u32[]{:S(2)}) copy-start(bf16[5,512]{1,0:T(8,128)(2,1)} %param.36) | copy-start | bytes 15364
  13.5 24.5 %copy-start.93 = (bf16[512]{0:T(512)(128)(2,1)S(1)}, bf16[512]{0:T(512)(128)(2,1)}, u32[]{:S(2)}) copy-start(bf16[512]{0:T(512)(128)(2,1)} %param.34) | copy-start | bytes 3076
  13.5 28.9 %copy-start.94 = (bf16[512]{0:T(512)(128)(2,1)S(1)}, bf16[512]{0:T(512)(128)(2,1)}, u32[]{:S(2)}) copy-start(bf16[512]{0:T(512)(128)(2,1)} %param.38) | copy-start | bytes 3076
  13.5 33.2 %copy-start.95 = (bf16[512]{0:T(512)(128)(2,1)S(1)}, bf16[512]{0:T(512)(128)(2,1)}, u32[]{:S(2)}) copy-start(bf16[512]{0:T(512)(128)(2,1)} %param.37) | copy-start | bytes 3076
  13.5 37.6 %copy-start.96 = (bf16[512]{0:T(512)(128)(2,1)S(1)}, bf16[512]{0:T(512)(128)(2,1)}, u32[]{:S(2)}) copy-start(bf16[512]{0:T(512)(128)(2,1)} %param.40) | copy-start | bytes 3076
  13.5 41.9 %copy-start.97 = (bf16[512]{0:T(512)(128)(2,1)S(1)}, bf16[512]{0:T(512)(128)(2,1)}, u32[]{:S(2)}) copy-start(bf16[512]{0:T(512)(128)(2,1)} %param.43) | copy-start | bytes 3076
  13.5 946.7 %reduce-scatter.17.cloned.1.call-start = ((), (), s32[]{:S(2)}) async-start(), calls=%async_computation.22 | async-start | bytes 3145728 | tf_op jit(solution)/shard_map/reduce_scatter | solution.py:351
  19.6 131.8 %copy-start.58 = (f32[2,1,512]{2,1,0:T(1,128)}, f32[2,1,512]{2,1,0:T(1,128)S(1)}, u32[]{:S(2)}) copy-start(f32[2,1,512]{2,1,0:T(1,128)S(1)} %convert_element_type.433) | copy-start | bytes 12292
  19.8 131.6 %copy-start.60 = (f32[512]{0:T(512)}, f32[512]{0:T(512)S(1)}, u32[]{:S(2)}) copy-start(f32[512]{0:T(512)S(1)} %broadcast_multiply_fusion.9) | copy-start | bytes 6148
  20.2 39.6 %copy-start.62 = (f32[512]{0:T(512)}, f32[512]{0:T(512)S(1)}, u32[]{:S(2)}) copy-start(f32[512]{0:T(512)S(1)} %fusion.22) | copy-start | bytes 6148
  20.2 131.2 %copy-start.64 = (f32[512]{0:T(512)}, f32[512]{0:T(512)S(1)}, u32[]{:S(2)}) copy-start(f32[512]{0:T(512)S(1)} %fusion.74) | copy-start | bytes 6148
  24.6 314.2 %copy-start.73 = (f32[2,1,512]{2,1,0:T(1,128)}, f32[2,1,512]{2,1,0:T(1,128)S(1)}, u32[]{:S(2)}) copy-start(f32[2,1,512]{2,1,0:T(1,128)S(1)} %convert_element_type.434) | copy-start | bytes 12292
  55.4 660.4 %copy-start.75 = (f32[2,1,512]{2,1,0:T(1,128)}, f32[2,1,512]{2,1,0:T(1,128)S(1)}, u32[]{:S(2)}) copy-start(f32[2,1,512]{2,1,0:T(1,128)S(1)} %convert_element_type.440) | copy-start | bytes 12292
  266.7 173.6 %copy-start.8 = (f32[512,1024]{1,0:T(8,128)}, f32[512,1024]{1,0:T(8,128)S(1)}, u32[]{:S(2)}) copy-start(f32[512,1024]{1,0:T(8,128)S(1)} %get-tuple-element.117) | copy-start | bytes 6291460
  266.7 77.9 %copy-start.66 = (f32[512]{0:T(512)}, f32[512]{0:T(512)S(1)}, u32[]{:S(2)}) copy-start(f32[512]{0:T(512)S(1)} %broadcast_multiply_fusion.8) | copy-start | bytes 6148
  267.0 77.5 %copy-start.70 = (f32[512]{0:T(512)}, f32[512]{0:T(512)S(1)}, u32[]{:S(2)}) copy-start(f32[512]{0:T(512)S(1)} %multiply_reduce_fusion.20) | copy-start | bytes 6148
  267.1 77.5 %copy-start.77 = (f32[512]{0:T(512)}, f32[512]{0:T(512)S(1)}, u32[]{:S(2)}) copy-start(f32[512]{0:T(512)S(1)} %fusion.75) | copy-start | bytes 6148
  499.5 216.3 %copy-start.68 = (f32[512]{0:T(512)}, f32[512]{0:T(512)S(1)}, u32[]{:S(2)}) copy-start(f32[512]{0:T(512)S(1)} %broadcast_multiply_fusion.6) | copy-start | bytes 6148
  501.2 214.6 %copy-start.79 = (f32[512]{0:T(512)}, f32[512]{0:T(512)S(1)}, u32[]{:S(2)}) copy-start(f32[512]{0:T(512)S(1)} %fusion.77) | copy-start | bytes 6148
  692.3 15.9 slice-start
  694.2 22.3 %copy-start.22 = (f32[512,1024]{1,0:T(8,128)}, f32[512,1024]{1,0:T(8,128)S(1)}, u32[]{:S(2)}) copy-start(f32[512,1024]{1,0:T(8,128)S(1)} %get-tuple-element.83) | copy-start | bytes 6291460
  694.3 22.3 %copy-start.81 = (f32[512]{0:T(512)}, f32[512]{0:T(512)S(1)}, u32[]{:S(2)}) copy-start(f32[512]{0:T(512)S(1)} %negate_multiply_fusion.4) | copy-start | bytes 6148
  694.3 13.9 copy-start.11
  694.3 13.9 slice-start.1
  718.1 4.4 copy-start.24
  771.6 6.8 copy-start.45
  771.7 6.8 copy-start.46
  810.4 11.3 copy-start.28
  827.3 133.0 %reduce-scatter.19.cloned.1.call-start = ((), (), s32[]{:S(2)}) async-start(), calls=%async_computation.23 | async-start | bytes 3145728 | tf_op jit(solution)/shard_map/reduce_scatter | solution.py:360
  832.9 127.4 %reduce-scatter.25.cloned.1.call-start = ((), (), s32[]{:S(2)}) async-start(), calls=%async_computation.26 | async-start | bytes 3145728 | tf_op jit(solution)/shard_map/reduce_scatter | solution.py:378
  837.4 148.1 %reduce-scatter.21.cloned.1.call-start = ((), (), s32[]{:S(2)}) async-start(), calls=%async_computation.24 | async-start | bytes 6291456 | tf_op jit(solution)/shard_map/reduce_scatter | solution.py:366
  845.7 219.7 %reduce-scatter.15.cloned.1.call-start = ((), (), s32[]{:S(2)}) async-start(), calls=%async_computation.21 | async-start | bytes 9437184 | tf_op jit(solution)/shard_map/reduce_scatter | solution.py:348
  889.3 7.2 copy-start.71
  889.3 278.1 %reduce-scatter.11.cloned.1.call-start = ((), (), s32[]{:S(2)}) async-start(), calls=%async_computation.19 | async-start | bytes 12582912 | tf_op jit(solution)/shard_map/reduce_scatter | solution.py:130
  898.4 22.0 %copy-start.16 = (f32[512,1024]{1,0:T(8,128)}, f32[512,1024]{1,0:T(8,128)S(1)}, u32[]{:S(2)}) copy-start(f32[512,1024]{1,0:T(8,128)S(1)} %add_add_fusion.5) | copy-start | bytes 6291460
  898.4 14.6 copy-start.7
  898.4 14.6 copy-start.59
  898.4 14.6 copy-start.61
  898.4 14.6 copy-start.65
  920.3 349.1 %reduce-scatter.13.cloned.1.call-start = ((), (), s32[]{:S(2)}) async-start(), calls=%async_computation.20 | async-start | bytes 12582912 | tf_op jit(solution)/shard_map/reduce_scatter | solution.py:133
  931.3 440.2 %reduce-scatter.27.cloned.1.call-start = ((), (), s32[]{:S(2)}) async-start(), calls=%async_computation.27 | async-start | bytes 12582912 | tf_op jit(solution)/shard_map/reduce_scatter | solution.py:130
  942.1 530.8 %reduce-scatter.29.cloned.1.call-start = ((), (), s32[]{:S(2)}) async-start(), calls=%async_computation.28 | async-start | bytes 12582912 | tf_op jit(solution)/shard_map/reduce_scatter | solution.py:133
  955.1 4.5 copy-start.72
  955.1 541.6 %reduce-scatter.23.cloned.1.call-start = ((), (), s32[]{:S(2)}) async-start(), calls=%async_computation.25 | async-start | bytes 24576 | tf_op jit(solution)/shard_map/reduce_scatter | solution.py:369
  960.2 981.9 %all-reduce.31.cloned.1.call-start = ((), (), s32[]{:S(2)}) async-start(), calls=%async_computation.29 | async-start | bytes 50331648 | tf_op jit(solution)/shard_map/psum | solution.py:389
  1474.9 8.5 copy-start.63
  1483.4 10.1 copy-start.17
  1942.1 6.8 copy-start.31
  1948.9 4.4 copy-start.43
  1960.8 4.4 copy-start.30
  1965.2 4.5 copy-start.29
  (62 other events, 132.9 us)
Sparse Core Ops, SparseCore 0:
  9.6 36.1 all-gather.24
  47.3 104.0 all-gather.18
  153.0 104.0 all-gather.20
  258.4 80.3 all-gather.22
  340.2 33.1 all-gather.26
  374.8 56.7 all-gather.28
  433.1 33.6 all-gather.30
  468.3 104.7 all-gather.32
  574.6 103.9 all-gather.34
  827.4 32.5 reduce-scatter.16
  862.4 31.8 reduce-scatter.18
  896.9 31.8 reduce-scatter.24
  931.2 54.3 reduce-scatter.20
  988.2 77.0 reduce-scatter.14
  1068.2 99.2 reduce-scatter.10
  1170.2 99.2 reduce-scatter.12
  1272.2 99.2 reduce-scatter.26
  1373.7 99.2 reduce-scatter.28
  1475.8 9.7 reduce-scatter.22
  1492.8 449.2 all-reduce.30
where the time goes:
time: 1990 us; the launch traced here: 1980 us
  waiting for transfers between devices  1310 us (66%)
  matrix products  230 us (12%)
  blocking collectives  195 us (10%)
  local copies, waits for them, and re-layouts  153 us (8%)
  other arithmetic  76.6 us (4%)
    psum x1, waiting for transfers between devices, on_device(): lax.psum(early_shards[1].astype(jnp.bfloat16), 'dp').astype(jnp.float32)  376 us
    dot_general x35, matrix products, product(): return jnp.einsum(form, left, right, preferred_element_type=jnp.float32)  230 us
    reduce_scatter x2, waiting for transfers between devices, ffn_backward(): lax.psum_scatter(grad_up.astype(jnp.bfloat16), 'fsdp', scatter_dimension=...  204 us
    reduce_scatter x2, waiting for transfers between devices, ffn_backward(): lax.psum_scatter(grad_down.astype(jnp.bfloat16), 'fsdp', scatter_dimensio...  203 us
    all_gather x2, waiting for transfers between devices, prepare_ffn(): lax.all_gather(down_weight, 'fsdp', axis=0, tiled=True)  188 us
    all_gather x2, waiting for transfers between devices, prepare_ffn(): lax.all_gather(up_weight, 'fsdp', axis=1, tiled=True)  154 us
    reduce_scatter x1, waiting for transfers between devices, on_device(): lax.psum_scatter(attend_grads[1].astype(jnp.bfloat16), 'fsdp', scatter_di...  79.8 us
    all_gather x1, waiting for transfers between devices, gather_attend(): lax.all_gather(heads_weight, 'fsdp', axis=0, tiled=True)  71.8 us
  transfers between devices with their start and end apart: 20, of which 12 were waited for; matrix products, arithmetic and copies ran while one was open for 15% of the time, Pallas kernels for 0%

commit v1 on v0

--- a/solution.py
+++ b/solution.py
@@ -1,11 +1,697 @@
+import functools
 import math
 
 import jax
 import jax.numpy as jnp
 from jax import lax
+from jax.experimental import pallas as pl
+from jax.experimental.pallas import tpu as pltpu
+from jax.sharding import Mesh
 from jax.sharding import PartitionSpec as P
 
 HEAD_DIM = 128
+F32 = jnp.float32
+BF16 = jnp.bfloat16
+SWAP = ((0, 1), (1, 0))
+Z_NEAR = ((0, 1), (1, 0), (2, 3), (3, 2))
+Z_FAR = ((0, 2), (2, 0), (1, 3), (3, 1))
+VMEM_LIMIT = 56 << 20
+
+
+def product(form, left, right):
+    return jnp.einsum(form, left, right, preferred_element_type=F32)
+
+
+def rows_of(array, start, size):
+    return lax.dynamic_slice_in_dim(array, start, size, 0)
+
+
+def cols_of(array, start, size):
+    return lax.dynamic_slice_in_dim(array, start, size, 1)
+
+
+def normalise(signal):
+    centred = signal - jnp.mean(signal, axis=-1, keepdims=True)
+    inverse = lax.rsqrt(jnp.mean(centred * centred, axis=-1, keepdims=True) + 1e-05)
+    return centred * inverse, inverse
+
+
+def norm_backward(signal, gain, upstream):
+    unit, inverse = normalise(signal)
+    scaled = upstream * gain
+    along = jnp.mean(scaled * unit, axis=-1, keepdims=True)
+    grad = inverse * (scaled - jnp.mean(scaled, axis=-1, keepdims=True) - unit * along)
+    return grad, jnp.sum(upstream * unit, axis=0)
+
+
+def silu_slope(value):
+    gate = jax.nn.sigmoid(value)
+    return gate * (1.0 + value * (1.0 - gate))
+
+
+def shifted(pieces, offset):
+    frames = pieces.shape[1]
+    if offset == 0:
+        return pieces
+    if offset > 0:
+        return jnp.pad(pieces[:, offset:], ((0, 0), (0, offset), (0, 0)))
+    return jnp.pad(pieces[:, : frames + offset], ((0, 0), (-offset, 0), (0, 0)))
+
+
+def sinusoid(rows, frames, model_width):
+    distance = (frames - 1 - jnp.arange(rows)).astype(F32)
+    halves = model_width // 2
+    frequency = jnp.exp(
+        jnp.arange(halves).astype(F32) * (-2.0 * math.log(10000.0) / model_width)
+    )
+    angles = distance[:, None] * frequency[None, :]
+    return jnp.concatenate([jnp.sin(angles), jnp.cos(angles)], axis=1)
+
+
+def head_columns(h, base=0):
+    return pl.ds(pl.multiple_of(base + h * HEAD_DIM, HEAD_DIM), HEAD_DIM)
+
+
+def dot(left, right, dims):
+    return lax.dot_general(left, right, (dims, ((), ())), preferred_element_type=F32)
+
+
+def attend_forward_body(lengths, joined, biases, relative, context, probs):
+    frames, width = context.shape
+    length = lengths[pl.program_id(0)]
+    scale = 1.0 / math.sqrt(HEAD_DIM)
+    key_index = lax.broadcasted_iota(jnp.int32, (frames, frames), 1)
+
+    def head(h, carry):
+        at = head_columns(h)
+        queries = joined[:, at]
+        keys = joined[:, head_columns(h, width)].astype(BF16)
+        values = joined[:, head_columns(h, 2 * width)].astype(BF16)
+        q_content = (queries + biases[0:1, at]).astype(BF16)
+        q_position = (queries + biases[1:2, at]).astype(BF16)
+        content = dot(q_content, keys, ((1,), (1,)))
+        spanning = dot(q_position, relative[:, at], ((1,), (1,)))
+        spanning = pltpu.roll(spanning, frames + 1, 1, stride=1, stride_axis=0)[:, :frames]
+        scores = jnp.where(key_index < length, (content + spanning) * scale, -1e30)
+        weights = jnp.exp(scores - jnp.max(scores, axis=-1, keepdims=True))
+        low = (weights / jnp.sum(weights, axis=-1, keepdims=True)).astype(BF16)
+        probs[0, h] = low
+        context[:, at] = dot(low, values, ((1,), (0,))).astype(BF16)
+        return carry
+
+    lax.fori_loop(0, width // HEAD_DIM, head, 0)
+
+
+def attend_backward_body(
+    joined, biases, relative, probs, grad_context, grad_joined, grad_relative, grad_biases
+):
+    frames, width = grad_context.shape
+    scale = 1.0 / math.sqrt(HEAD_DIM)
+    row = lax.broadcasted_iota(jnp.int32, (frames, frames), 0)
+    column = lax.broadcasted_iota(jnp.int32, (frames, frames), 1)
+    flip = jnp.where(row + column == frames - 1, 1.0, 0.0).astype(BF16)
+
+    @pl.when(pl.program_id(0) == 0)
+    def _():
+        grad_relative[...] = jnp.zeros_like(grad_relative)
+        grad_biases[...] = jnp.zeros_like(grad_biases)
+
+    def head(h, carry):
+        at = head_columns(h)
+        queries = joined[:, at]
+        keys = joined[:, head_columns(h, width)].astype(BF16)
+        values = joined[:, head_columns(h, 2 * width)].astype(BF16)
+        q_content = (queries + biases[0:1, at]).astype(BF16)
+        q_position = (queries + biases[1:2, at]).astype(BF16)
+        low = probs[0, h]
+        weights = low.astype(F32)
+        upstream = grad_context[:, at]
+        grad_probs = dot(upstream, values, ((1,), (1,)))
+        grad_values = dot(low, upstream, ((0,), (0,)))
+        inner = jnp.sum(grad_probs * weights, axis=-1, keepdims=True)
+        grad_raw = (weights * (grad_probs - inner) * scale).astype(BF16)
+        grad_keys = dot(grad_raw, q_content, ((0,), (0,)))
+        turned = dot(flip, grad_raw, ((1,), (0,))).astype(BF16)
+        q_turned = dot(flip, q_position, ((1,), (0,))).astype(BF16)
+        wide = jnp.concatenate([turned, jnp.zeros_like(turned)], axis=1)
+        wide = pltpu.roll(wide, 0, 1, stride=1, stride_axis=0)
+        grad_content = dot(turned, keys, ((1,), (0,)))
+        grad_position = dot(wide, relative[:, at], ((1,), (0,)))
+        grad_queries = (grad_content + grad_position).astype(BF16)
+        grad_relative[:, at] += dot(wide, q_turned, ((0,), (0,)))
+        grad_biases[0:1, at] += jnp.sum(grad_content, axis=0, keepdims=True)
+        grad_biases[1:2, at] += jnp.sum(grad_position, axis=0, keepdims=True)
+        grad_joined[:, at] = dot(flip, grad_queries, ((1,), (0,))).astype(BF16)
+        grad_joined[:, head_columns(h, width)] = grad_keys.astype(BF16)
+        grad_joined[:, head_columns(h, 2 * width)] = grad_values.astype(BF16)
+        return carry
+
+    lax.fori_loop(0, width // HEAD_DIM, head, 0)
+
+
+def attend_forward(joined, biases, relative, lengths):
+    utterances = lengths.shape[0]
+    frames = joined.shape[0] // utterances
+    width = relative.shape[1]
+    heads = width // HEAD_DIM
+    return pl.pallas_call(
+        attend_forward_body,
+        grid_spec=pltpu.PrefetchScalarGridSpec(
+            num_scalar_prefetch=1,
+            grid=(utterances,),
+            in_specs=[
+                pl.BlockSpec((frames, 3 * width), lambda u, n: (u, 0)),
+                pl.BlockSpec((2, width), lambda u, n: (0, 0)),
+                pl.BlockSpec((2 * frames, width), lambda u, n: (0, 0)),
+            ],
+            out_specs=[
+                pl.BlockSpec((frames, width), lambda u, n: (u, 0)),
+                pl.BlockSpec((1, heads, frames, frames), lambda u, n: (u, 0, 0, 0)),
+            ],
+        ),
+        out_shape=[
+            jax.ShapeDtypeStruct((utterances * frames, width), BF16),
+            jax.ShapeDtypeStruct((utterances, heads, frames, frames), BF16),
+        ],
+        compiler_params=pltpu.CompilerParams(vmem_limit_bytes=VMEM_LIMIT),
+        cost_estimate=pl.CostEstimate(
+            flops=10 * utterances * frames * frames * width,
+            bytes_accessed=joined.size * 4 + utterances * frames * width * 4,
+            transcendentals=utterances * heads * frames * frames,
+        ),
+        name="attend_forward",
+    )(lengths, joined, biases, relative)
+
+
+def attend_backward(joined, biases, relative, probs, grad_context):
+    utterances, heads, frames, _ = probs.shape
+    width = relative.shape[1]
+    return pl.pallas_call(
+        attend_backward_body,
+        grid=(utterances,),
+        in_specs=[
+            pl.BlockSpec((frames, 3 * width), lambda u: (u, 0)),
+            pl.BlockSpec((2, width), lambda u: (0, 0)),
+            pl.BlockSpec((2 * frames, width), lambda u: (0, 0)),
+            pl.BlockSpec((1, heads, frames, frames), lambda u: (u, 0, 0, 0)),
+            pl.BlockSpec((frames, width), lambda u: (u, 0)),
+        ],
+        out_specs=[
+            pl.BlockSpec((frames, 3 * width), lambda u: (u, 0)),
+            pl.BlockSpec((2 * frames, width), lambda u: (0, 0)),
+            pl.BlockSpec((2, width), lambda u: (0, 0)),
+        ],
+        out_shape=[
+            jax.ShapeDtypeStruct((utterances * frames, 3 * width), BF16),
+            jax.ShapeDtypeStruct((2 * frames, width), F32),
+            jax.ShapeDtypeStruct((2, width), F32),
+        ],
+        compiler_params=pltpu.CompilerParams(vmem_limit_bytes=VMEM_LIMIT),
+        cost_estimate=pl.CostEstimate(
+            flops=24 * utterances * frames * frames * width,
+            bytes_accessed=joined.size * 8,
+            transcendentals=0,
+        ),
+        name="attend_backward",
+    )(joined, biases, relative, probs, grad_context)
+
+
+def place_body(count, block_rows, where, *refs):
+    sources, target, held, arrived, left = refs[:count], refs[count], *refs[count + 1 :]
+    copies = []
+    for source in sources:
+        for block in range(source.shape[0] // block_rows):
+            slot = len(copies)
+            start = pl.multiple_of(where[slot] * block_rows, block_rows)
+            rows = pl.ds(slot * block_rows, block_rows)
+            copies.append(
+                (
+                    pltpu.make_async_copy(
+                        source.at[pl.ds(block * block_rows, block_rows)],
+                        held.at[rows],
+                        arrived.at[slot],
+                    ),
+                    pltpu.make_async_copy(
+                        held.at[rows], target.at[pl.ds(start, block_rows)], left.at[slot]
+                    ),
+                )
+            )
+    for fetch, _ in copies:
+        fetch.start()
+    for fetch, store in copies:
+        fetch.wait()
+        store.start()
+    for _, store in copies:
+        store.wait()
+
+
+def place(sources, block_rows, where, rows):
+    blocks = rows // block_rows
+    width = sources[0].shape[1]
+    return pl.pallas_call(
+        functools.partial(place_body, len(sources), block_rows),
+        grid_spec=pltpu.PrefetchScalarGridSpec(
+            num_scalar_prefetch=1,
+            grid=(1,),
+            in_specs=[pl.BlockSpec(memory_space=pl.ANY)] * len(sources),
+            out_specs=pl.BlockSpec(memory_space=pl.ANY),
+            scratch_shapes=[
+                pltpu.VMEM((rows, width), sources[0].dtype),
+                pltpu.SemaphoreType.DMA((blocks,)),
+                pltpu.SemaphoreType.DMA((blocks,)),
+            ],
+        ),
+        out_shape=jax.ShapeDtypeStruct((rows, width), sources[0].dtype),
+        compiler_params=pltpu.CompilerParams(vmem_limit_bytes=VMEM_LIMIT),
+        cost_estimate=pl.CostEstimate(
+            flops=0, bytes_accessed=4 * rows * width, transcendentals=0
+        ),
+        name="place",
+    )(where, *sources)
+
+
+def widen_body(spans, by_rows, where, *refs):
+    count = len(spans)
+    sources, targets = refs[:4], refs[4 : 4 + count]
+    held, wide, arrived, left = refs[4 + count :]
+    rows = held.shape[1]
+    block = rows // 4
+    fetches = [
+        pltpu.make_async_copy(sources[k], held.at[k], arrived.at[k]) for k in range(4)
+    ]
+    for fetch in fetches:
+        fetch.start()
+    stores = []
+    for k in range(4):
+        fetches[k].wait()
+        for b in range(4):
+            at = pl.ds(k * rows + b * block, block)
+            wide[at, :] = held[k, b * block : (b + 1) * block].astype(F32)
+            spot = where[4 * k + b]
+            for n, ((start, span), target) in enumerate(zip(spans, targets)):
+                if by_rows:
+                    into = target.at[pl.ds(pl.multiple_of(spot * block, block), block)]
+                else:
+                    row = pl.multiple_of(lax.rem(spot, 8) * block, block)
+                    column = pl.multiple_of((spot // 8) * span, HEAD_DIM)
+                    into = target.at[pl.ds(row, block), pl.ds(column, span)]
+                store = pltpu.make_async_copy(
+                    wide.at[at, pl.ds(start, span)], into, left.at[len(stores)]
+                )
+                store.start()
+                stores.append(store)
+    for store in stores:
+        store.wait()
+
+
+def widen(sources, spans, where, by_rows):
+    rows, width = sources[0].shape
+    if by_rows:
+        shards = [jax.ShapeDtypeStruct((4 * rows, span), F32) for _, span in spans]
+    else:
+        shards = [jax.ShapeDtypeStruct((2 * rows, 2 * span), F32) for _, span in spans]
+    return pl.pallas_call(
+        functools.partial(widen_body, spans, by_rows),
+        grid_spec=pltpu.PrefetchScalarGridSpec(
+            num_scalar_prefetch=1,
+            grid=(1,),
+            in_specs=[pl.BlockSpec(memory_space=pl.ANY)] * 4,
+            out_specs=[pl.BlockSpec(memory_space=pl.ANY)] * len(spans),
+            scratch_shapes=[
+                pltpu.VMEM((4, rows, width), BF16),
+                pltpu.VMEM((4 * rows, width), F32),
+                pltpu.SemaphoreType.DMA((4,)),
+                pltpu.SemaphoreType.DMA((16 * len(spans),)),
+            ],
+        ),
+        out_shape=shards,
+        compiler_params=pltpu.CompilerParams(vmem_limit_bytes=VMEM_LIMIT),
+        cost_estimate=pl.CostEstimate(
+            flops=0, bytes_accessed=4 * rows * width * 6, transcendentals=0
+        ),
+        name="widen",
+    )(where, *sources)
+
+
+class PairPlan:
+    axes = ("z", "y", "c", "x")
+
+    def __init__(self):
+        self.z, self.y, self.c, self.x = (lax.axis_index(name) for name in self.axes)
+        self.near = lax.rem(self.z, 2)
+        self.far = self.z // 2
+
+    def over(self, name, value):
+        return lax.ppermute(value, name, SWAP)
+
+    def over_near(self, value):
+        return lax.ppermute(value, "z", Z_NEAR)
+
+    def over_far(self, value):
+        return lax.ppermute(value, "z", Z_FAR)
+
+    def total(self, value):
+        value = value + self.over("c", value)
+        diagonal = ((0, 3), (3, 0), (1, 2), (2, 1))
+        value = (value + self.over("x", value)) + (
+            self.over("y", value) + lax.ppermute(value, ("y", "x"), diagonal)
+        )
+        turned = [
+            lax.ppermute(value, "z", tuple((i, (i + k) % 4) for i in range(4))) for k in (1, 2, 3)
+        ]
+        return (value + turned[1]) + (turned[0] + turned[2])
+
+    def whole_vectors(self, stacked):
+        other = self.over("x", stacked)
+        low = jnp.where(self.x == 0, stacked, other)
+        high = jnp.where(self.x == 0, other, stacked)
+        return jnp.concatenate([low, high], axis=1)
+
+    def fetch(self, shard, y_first):
+        eighth = shard.shape[0] // 8
+        mine = self.c * 4 + self.y * 2 + self.near
+        piece = self.over("x", rows_of(shard, mine * eighth, eighth))
+        if y_first:
+            both = jnp.concatenate([piece, self.over("y", piece)], axis=0)
+            others = self.over_near(both)
+            flips = (0, 2, 1, 3)
+        else:
+            both = jnp.concatenate([piece, self.over_near(piece)], axis=0)
+            others = self.over("y", both)
+            flips = (0, 1, 2, 3)
+        sources = (both, others, self.over("c", both), self.over("c", others))
+        inner = self.y * 2 + self.near
+        places = [jnp.bitwise_xor(inner, flip) for flip in flips]
+        places = [self.c * 4 + k for k in places] + [(1 - self.c) * 4 + k for k in places]
+        return sources, places, eighth
+
+    def other_shard(self, shard, y_first):
+        sources, places, eighth = self.fetch(shard, y_first)
+        return place(sources, eighth, jnp.stack(places), shard.shape[0])
+
+    def whole_rows(self, shard, y_first):
+        sources, places, eighth = self.fetch(shard, y_first)
+        places = [(1 - self.x) * 8 + k for k in places] + [self.x * 8 + k for k in range(8)]
+        return place(sources + (shard,), eighth, jnp.stack(places), 2 * shard.shape[0])
+
+    def pairs(self, up, down):
+        return [(up, down), (self.other_shard(up, True), self.other_shard(down, False))]
+
+    def with_core(self, value):
+        return jnp.concatenate([value, self.over("c", value)], axis=0)
+
+    def with_core_half(self, value):
+        half = value.shape[1] // 2
+        sent = self.over("c", cols_of(value, (1 - self.c) * half, half))
+        return jnp.concatenate([cols_of(value, self.c * half, half), sent], axis=0)
+
+    def summed(self, keep, send, spans, by_rows):
+        half = keep.shape[0] // 2
+        quarter, eighth = half // 2, half // 4
+
+        def cut(value, start, size):
+            return rows_of(value, start, size).astype(F32)
+
+        met = self.over("x", send)
+        away = (1 - self.y) * half
+        sent = (cut(keep, away, half) + cut(met, away, half)).astype(BF16)
+        mine = cut(keep, self.y * half, half) + cut(met, self.y * half, half)
+        mine = mine + self.over("y", sent).astype(F32)
+        sent = rows_of(mine, (1 - self.near) * quarter, quarter).astype(BF16)
+        mine = rows_of(mine, self.near * quarter, quarter) + self.over_near(sent).astype(F32)
+        sent = rows_of(mine, (1 - self.far) * eighth, eighth).astype(BF16)
+        mine = rows_of(mine, self.far * eighth, eighth) + self.over_far(sent).astype(F32)
+        mine = mine.astype(BF16)
+        line = jnp.concatenate([mine, self.over_far(mine)], axis=0)
+        line = jnp.concatenate([line, self.over_near(line)], axis=0)
+        other = self.over("y", line)
+        sources = (line, other, self.over("c", line), self.over("c", other))
+        places = []
+        for c in (self.c, 1 - self.c):
+            for y in (self.y, 1 - self.y):
+                for near in (self.near, 1 - self.near):
+                    for far in (self.far, 1 - self.far):
+                        places.append(c * 8 + y * 4 + near * 2 + far)
+        return widen(sources, spans, jnp.stack(places), by_rows)
+
+
+def split_sizes(array, sizes):
+    out, start = [], 0
+    for size in sizes:
+        out.append(array[:, start : start + size])
+        start += size
+    return out
+
+
+def pair_layer(*arguments):
+    (
+        tokens,
+        lengths,
+        cotangent,
+        early_norm,
+        early_up,
+        early_down,
+        attend_norm,
+        heads_weight,
+        position_weight,
+        content_bias,
+        position_bias,
+        attend_output,
+        mixer_norm,
+        gating_weight,
+        depth_kernel,
+        batch_gain,
+        batch_shift,
+        mixer_output,
+        late_norm,
+        late_up,
+        late_down,
+        final_gain,
+    ) = arguments
+    plan = PairPlan()
+    utterances = lengths.shape[0]
+    rows, width = tokens.shape
+    frames = rows // utterances
+    taps = depth_kernel.shape[0]
+    middle = (taps - 1) // 2
+    mask = (lax.iota(jnp.int32, frames)[None, :] < lengths[:, None]).reshape(rows, 1).astype(F32)
+
+    early = plan.pairs(early_up, early_down)
+    vectors = jnp.stack(
+        [
+            early_norm,
+            attend_norm,
+            mixer_norm,
+            late_norm,
+            final_gain,
+            content_bias,
+            position_bias,
+            batch_gain,
+            batch_shift,
+        ]
+    )
+    vectors = plan.whole_vectors(jnp.concatenate([vectors, depth_kernel], axis=0)).astype(F32)
+    early_norm, attend_norm, mixer_norm, late_norm, final_gain = vectors[0:5]
+    biases = vectors[5:7]
+    batch_gain, batch_shift = vectors[7:9]
+    depth_kernel = vectors[9:]
+    attend_packed = plan.whole_rows(
+        jnp.concatenate([heads_weight, position_weight, attend_output], axis=1), True
+    )
+    heads_weight, position_weight, attend_output = split_sizes(
+        attend_packed, (3 * width, width, width)
+    )
+    mixer_packed = plan.whole_rows(jnp.concatenate([gating_weight, mixer_output], axis=1), False)
+    gating_weight, mixer_output = split_sizes(mixer_packed, (2 * width, width))
+    late = plan.pairs(late_up, late_down)
+
+    def ffn_forward(signal, gain, parts):
+        normed = (normalise(signal)[0] * gain).astype(BF16)
+        hidden = [product("td,df->tf", normed, up) for up, _ in parts]
+        active = [jax.nn.silu(value).astype(BF16) for value in hidden]
+        total = sum(product("tf,fd->td", a, down) for a, (_, down) in zip(active, parts))
+        return signal + 0.5 * total, (signal, normed, hidden, active)
+
+    def ffn_backward(saved, gain, parts, upstream):
+        signal, normed, hidden, active = saved
+        out_grad = (0.5 * upstream).astype(BF16)
+        grad_hidden = [
+            (product("td,fd->tf", out_grad, down) * silu_slope(value)).astype(BF16)
+            for value, (_, down) in zip(hidden, parts)
+        ]
+        both_out = plan.with_core(out_grad)
+        grad_downs = [
+            product("tf,td->fd", plan.with_core_half(a), both_out).astype(BF16) for a in active
+        ]
+        grad_downs, grad_hidden = lax.optimization_barrier((grad_downs, grad_hidden))
+        down_shard = plan.summed(grad_downs[0], grad_downs[1], ((0, width),), True)[0]
+        both_normed = plan.with_core(normed)
+        grad_ups = [
+            product("td,tf->df", both_normed, plan.with_core_half(g)).astype(BF16)
+            for g in grad_hidden
+        ]
+        grad_ups, grad_hidden = lax.optimization_barrier((grad_ups, grad_hidden))
+        half = grad_ups[0].shape[1]
+        up_shard = plan.summed(grad_ups[0], grad_ups[1], ((0, half),), False)[0]
+        grad_normed = sum(product("tf,df->td", g, up) for g, (up, _) in zip(grad_hidden, parts))
+        grad_signal, grad_gain = norm_backward(signal, gain, grad_normed)
+        return upstream + grad_signal, grad_gain, up_shard, down_shard
+
+    start = tokens.astype(F32)
+    after_early, early_saved = ffn_forward(start, early_norm, early)
+
+    att_normed = (normalise(after_early)[0] * attend_norm).astype(BF16)
+    joined = product("td,de->te", att_normed, heads_weight)
+    table = sinusoid(2 * frames, frames, width).astype(BF16)
+    relative = product("nc,cd->nd", table, position_weight).astype(BF16)
+    context, probs = attend_forward(joined, biases, relative, lengths)
+    after_attend = after_early + product("td,de->te", context, attend_output)
+
+    mix_normed = (normalise(after_attend)[0] * mixer_norm).astype(BF16)
+    gate_joined = product("td,de->te", mix_normed, gating_weight)
+    linear, gate = gate_joined[:, :width], jax.nn.sigmoid(gate_joined[:, width:])
+    slots = (utterances, frames, width)
+    gated = (linear * gate * mask).reshape(slots)
+    mixed = sum(shifted(gated, k - middle) * depth_kernel[k] for k in range(taps))
+    mixed = mixed.reshape(rows, width)
+    masked = mixed * mask
+    counts = jnp.full((1, width), 1.0, F32) * jnp.sum(mask)
+    moments = jnp.concatenate(
+        [
+            jnp.sum(masked, axis=0, keepdims=True),
+            jnp.sum(masked * mixed, axis=0, keepdims=True),
+            counts,
+        ],
+        axis=0,
+    )
+    moments = plan.total(moments)
+    frames_total = moments[2]
+    average = moments[0] / frames_total
+    inv_scale = lax.rsqrt(moments[1] / frames_total - average * average + 1e-05)
+    bn_out = (mixed - average) * inv_scale * batch_gain + batch_shift
+    mix_active = jax.nn.silu(bn_out).astype(BF16)
+    after_mixer = after_attend + product("td,de->te", mix_active, mixer_output)
+
+    after_late, late_saved = ffn_forward(after_mixer, late_norm, late)
+    unit, _ = normalise(after_late)
+    output = (unit * final_gain).astype(BF16)
+
+    upstream, grad_final = norm_backward(
+        after_late, final_gain, cotangent.astype(F32) * mask
+    )
+    upstream, grad_late_norm, late_up_shard, late_down_shard = ffn_backward(
+        late_saved, late_norm, late, upstream
+    )
+
+    mix_out_grad = upstream.astype(BF16)
+    grad_bn = product("te,de->td", mix_out_grad, mixer_output) * silu_slope(bn_out)
+    unit_mixed = (mixed - average) * inv_scale
+    bn_sums = plan.total(
+        jnp.stack([jnp.sum(grad_bn * unit_mixed, axis=0), jnp.sum(grad_bn, axis=0)])
+    )
+    grad_gain, grad_shift = bn_sums[0], bn_sums[1]
+    grad_average = -grad_shift * inv_scale * batch_gain
+    grad_inv = grad_gain * batch_gain / inv_scale
+    sec_grad = -0.5 * inv_scale * inv_scale * inv_scale * grad_inv / frames_total
+    first_grad = grad_average / frames_total - 2.0 * average * sec_grad
+    grad_mixed = grad_bn * inv_scale * batch_gain + mask * (first_grad + 2.0 * mixed * sec_grad)
+    grad_mixed = grad_mixed.reshape(slots)
+    grad_gated = sum(shifted(grad_mixed, middle - k) * depth_kernel[k] for k in range(taps))
+    grad_depth = [
+        jnp.sum(grad_mixed * shifted(gated, k - middle), axis=(0, 1)) for k in range(taps)
+    ]
+    grad_gated = grad_gated.reshape(rows, width) * mask
+    grad_gate_joined = jnp.concatenate(
+        [grad_gated * gate, grad_gated * linear * gate * (1.0 - gate)], axis=1
+    ).astype(BF16)
+    half = width // 2
+    mix_half = plan.with_core_half(mix_out_grad)
+    both_active = plan.with_core(mix_active)
+    both_mix = plan.with_core(mix_normed)
+    gate_half = plan.with_core_half(grad_gate_joined)
+    mixer_blocks = jnp.concatenate(
+        [product("td,te->de", both_mix, gate_half), product("td,te->de", both_active, mix_half)],
+        axis=1,
+    ).astype(BF16)
+    mixer_blocks, grad_gate_joined = lax.optimization_barrier((mixer_blocks, grad_gate_joined))
+    gating_shard, mixer_output_shard = plan.summed(
+        rows_of(mixer_blocks, plan.x * half, half),
+        rows_of(mixer_blocks, (1 - plan.x) * half, half),
+        ((0, width), (width, half)),
+        False,
+    )
+    grad_normed = product("te,de->td", grad_gate_joined, gating_weight)
+    grad_signal, grad_mixer_norm = norm_backward(after_attend, mixer_norm, grad_normed)
+    upstream = upstream + grad_signal
+
+    att_out_grad = upstream.astype(BF16)
+    grad_context = product("te,de->td", att_out_grad, attend_output).astype(BF16)
+    grad_joined, grad_relative, grad_biases = attend_backward(
+        joined, biases, relative, probs, grad_context
+    )
+    grad_relative = grad_relative.astype(BF16)
+    relative_half = cols_of(grad_relative, plan.c * half, half).astype(F32) + plan.over(
+        "c", cols_of(grad_relative, (1 - plan.c) * half, half)
+    ).astype(F32)
+    attend_blocks = jnp.concatenate(
+        [
+            product("td,te->de", plan.with_core(att_normed), plan.with_core_half(grad_joined)),
+            product("nc,nd->cd", table, relative_half.astype(BF16)),
+            product("td,te->de", plan.with_core(context), plan.with_core_half(att_out_grad)),
+        ],
+        axis=1,
+    ).astype(BF16)
+    attend_blocks, grad_joined = lax.optimization_barrier((attend_blocks, grad_joined))
+    heads_shard, position_shard, attend_output_shard = plan.summed(
+        rows_of(attend_blocks, plan.x * half, half),
+        rows_of(attend_blocks, (1 - plan.x) * half, half),
+        ((0, 3 * half), (3 * half, half), (4 * half, half)),
+        False,
+    )
+    grad_normed = product("te,de->td", grad_joined, heads_weight)
+    grad_signal, grad_attend_norm = norm_backward(after_early, attend_norm, grad_normed)
+    upstream = upstream + grad_signal
+
+    upstream, grad_early_norm, early_up_shard, early_down_shard = ffn_backward(
+        early_saved, early_norm, early, upstream
+    )
+    small = jnp.stack(
+        [
+            grad_early_norm,
+            grad_attend_norm,
+            grad_biases[0],
+            grad_biases[1],
+            grad_mixer_norm,
+            grad_late_norm,
+            grad_final,
+        ]
+        + grad_depth
+    )
+    small = plan.total(small)
+    small = cols_of(jnp.concatenate([small, bn_sums], axis=0), plan.x * half, half)
+    return (
+        output,
+        upstream.astype(BF16),
+        small[0],
+        early_up_shard,
+        early_down_shard,
+        small[1],
+        heads_shard,
+        position_shard,
+        small[2],
+        small[3],
+        attend_output_shard,
+        small[4],
+        gating_shard,
+        small[7 : 7 + taps],
+        small[7 + taps],
+        small[8 + taps],
+        mixer_output_shard,
+        small[5],
+        late_up_shard,
+        late_down_shard,
+        small[6],
+    )
 
 
 def layer_norm(signal, norm_gain):
@@ -54,7 +740,7 @@
     return flat.reshape(head_count, frames, span_width - 1)[:, :, :frames]
 
 
-def sinusoid(frames, model_width):
+def distances(frames, model_width):
     distance = (frames - 1 - jnp.arange(2 * frames - 1)).astype(jnp.float32)
     halves = model_width // 2
     frequency = jnp.exp(
@@ -62,10 +748,6 @@
     )
     angles = distance[:, None] * frequency[None, :]
     return jnp.concatenate([jnp.sin(angles), jnp.cos(angles)], axis=1)
-
-
-def product(form, left, right):
-    return jnp.einsum(form, left, right, preferred_element_type=jnp.float32)
 
 
 def prepare_ffn(norm_gain, up_weight, down_weight):
@@ -273,7 +955,7 @@
     )
 
 
-def on_device(
+def any_layer(
     tokens,
     lengths,
     cotangent,
@@ -301,7 +983,7 @@
     frames = tokens.shape[0] // utterances
     key_valid = lax.iota(jnp.int32, frames)[None, :] < lengths[:, None]
     frame_mask = key_valid.reshape(-1, 1).astype(jnp.float32)
-    table = sinusoid(frames, tokens.shape[1]).astype(jnp.bfloat16)
+    table = distances(frames, tokens.shape[1]).astype(jnp.bfloat16)
     start = tokens.astype(jnp.float32)
     early = prepare_ffn(early_norm, early_up, early_down)
     after_early = ffn_forward(start, early)
@@ -430,54 +1112,50 @@
     )
 
 
+def pair_mesh(mesh):
+    if dict(mesh.shape) != {"dp": 16, "fsdp": 2}:
+        return None
+    return Mesh(mesh.devices.reshape(4, 2, 2, 2), PairPlan.axes)
+
+
+def spec(mesh, *dims):
+    names = {"dp": ("z", "y", "c"), "fsdp": ("x",)}
+    if "dp" in mesh.shape:
+        names = {"dp": ("dp",), "fsdp": ("fsdp",)}
+    return P(*[None if dim is None else sum((names[d] for d in dim), ()) for dim in dims])
+
+
 def solution(mesh):
-    in_specs = (
-        P(("dp", "fsdp"), None),
-        P(("dp", "fsdp")),
-        P(("dp", "fsdp"), None),
-        P("fsdp"),
-        P(None, "fsdp"),
-        P("fsdp", None),
-        P("fsdp"),
-        P("fsdp", None),
-        P("fsdp", None),
-        P("fsdp"),
-        P("fsdp"),
-        P("fsdp", None),
-        P("fsdp"),
-        P("fsdp", None),
-        P(None, "fsdp"),
-        P("fsdp"),
-        P("fsdp"),
-        P("fsdp", None),
-        P("fsdp"),
-        P(None, "fsdp"),
-        P("fsdp", None),
-        P("fsdp"),
-    )
-    out_specs = (
-        P(("dp", "fsdp"), None),
-        P(("dp", "fsdp"), None),
-        P("fsdp"),
-        P(None, "fsdp"),
-        P("fsdp", None),
-        P("fsdp"),
-        P("fsdp", None),
-        P("fsdp", None),
-        P("fsdp"),
-        P("fsdp"),
-        P("fsdp", None),
-        P("fsdp"),
-        P("fsdp", None),
-        P(None, "fsdp"),
-        P("fsdp"),
-        P("fsdp"),
-        P("fsdp", None),
-        P("fsdp"),
-        P(None, "fsdp"),
-        P("fsdp", None),
-        P("fsdp"),
+    inner = pair_mesh(mesh)
+    layer = any_layer if inner is None else pair_layer
+    inner = mesh if inner is None else inner
+    all_rows, vector = spec(inner, ("dp", "fsdp"), None), spec(inner, ("fsdp",))
+    by_rows, by_cols = spec(inner, ("fsdp",), None), spec(inner, None, ("fsdp",))
+    weights = (
+        vector,
+        by_cols,
+        by_rows,
+        vector,
+        by_rows,
+        by_rows,
+        vector,
+        vector,
+        by_rows,
+        vector,
+        by_rows,
+        by_cols,
+        vector,
+        vector,
+        by_rows,
+        vector,
+        by_cols,
+        by_rows,
+        vector,
     )
     return jax.shard_map(
-        on_device, mesh=mesh, in_specs=in_specs, out_specs=out_specs, check_vma=False
-    )
+        layer,
+        mesh=inner,
+        in_specs=(all_rows, spec(inner, ("dp", "fsdp")), all_rows) + weights,
+        out_specs=(all_rows, all_rows) + weights,
+        check_vma=False,
+    )

time: 1990 us -> 964 us (0.48)
  waiting for transfers between devices: 1310 us -> 437 us
  blocking collectives: 195 us -> 0 us
  starting transfers between devices: 1.59 us -> 112 us
  Pallas kernels: 0 us -> 99.2 us
  local copies, waits for them, and re-layouts: 153 us -> 66.3 us
  matrix products: 230 us -> 170 us
    reduce_scatter x10 -> x0, waiting for transfers between devices: 513 us -> none  [the longest x2 204 us: ffn_backward(): lax.psum_scatter(grad_up.astype(jnp.bfloat16), 'fsdp', scatter_dimension=...]
    ppermute x0 -> x127, waiting for transfers between devices: none -> 437 us  [the longest x85 173 us: over(): return lax.ppermute(value, name, SWAP)]
    all_gather x9 -> x0, waiting for transfers between devices: 414 us -> none  [the longest x2 188 us: prepare_ffn(): lax.all_gather(down_weight, 'fsdp', axis=0, tiled=True)]
    psum x1 -> x0, waiting for transfers between devices: 376 us -> none  [on_device(): lax.psum(early_shards[1].astype(jnp.bfloat16), 'dp').astype(jnp.float32)]
    psum x3 -> x0, blocking collectives: 143 us -> none  [the longest x1 63.4 us: on_device(): lax.psum(early_shards[0].astype(jnp.bfloat16), 'dp').astype(jnp.float32)]
    ppermute x0 -> x127, starting transfers between devices: none -> 112 us  [the longest x85 60.1 us: over(): return lax.ppermute(value, name, SWAP)]
    pallas_call x0 -> x14, Pallas kernels: none -> 99.2 us  [the longest x6 32.6 us: widen(): pl.pallas_call(functools.partial(widen_body, spans, by_rows), grid_spec=p...]
    dot_general x35 -> x38, matrix products: 230 us -> 170 us  [product(): return jnp.einsum(form, left, right, preferred_element_type=F32)]
  transfers between devices with their start and end apart: 20 -> 127, of which waited for: 12 -> 49; matrix products, arithmetic and copies ran while one was open for 15% -> 26% of each run, Pallas kernels for 0% -> 10%
where the time goes in v1:
time: 964 us; the launch traced here: 959 us
  waiting for transfers between devices  437 us (45%)
  matrix products  170 us (18%)
  starting transfers between devices  112 us (12%)
  Pallas kernels  99.2 us (10%)
  other arithmetic  72 us (7%)
  local copies, waits for them, and re-layouts  66.3 us (7%)
    ppermute x85, waiting for transfers between devices, over(): return lax.ppermute(value, name, SWAP)  173 us
    dot_general x38, matrix products, product(): return jnp.einsum(form, left, right, preferred_element_type=F32)  170 us
    ppermute x18, waiting for transfers between devices, over_near(): return lax.ppermute(value, 'z', Z_NEAR)  115 us
    ppermute x12, waiting for transfers between devices, over_far(): return lax.ppermute(value, 'z', Z_FAR)  93.5 us
    ppermute x85, starting transfers between devices, over(): return lax.ppermute(value, name, SWAP)  60.1 us
    ppermute x3, waiting for transfers between devices, total(): lax.ppermute(value, ('y', 'x'), diagonal)  41 us
    pallas_call x6, Pallas kernels, widen(): pl.pallas_call(functools.partial(widen_body, spans, by_rows), grid_spec=p...  32.6 us
    unnamed x254, local copies, waits for them, and re-layouts  32.5 us
  transfers between devices with their start and end apart: 127, of which 49 were waited for; matrix products, arithmetic and copies ran while one was open for 26% of the time, Pallas kernels for 10%

profile of v1, /device:TPU:0, one launch (start us, length us, event | category | flops | bytes accessed | tf_op | source)
XLA Modules:
  0.0 959.1 jit_solution(7808421215602866185)
XLA Ops:
  33.1 5.2 fusion.142
  46.3 7.4 multiply_convert_fusion.7
  68.4 5.1 collective-permute-done.28
  77.9 5.5 collective-permute-done.33
  86.5 25.5 %collective-permute-done.7 = bf16[256,1024]{1,0:T(8,128)(2,1)S(1)} collective-permute-done((bf16[256,1024]{1,0:T(8,128)(2,1)}, bf16[256,1024]{1,0:T(8,128)(2,1)S(1)}, u32[]{:S(2)}, u32[]{:S(2)}) %collective-permute-start.7) | collective-permute-done | bytes 524320 | tf_op jit(solution)/shard_map/ppermute | solution.py:348
  114.5 5.2 collective-permute-done.34
  127.9 19.2 %collective-permute-done.8.refs_1_ = bf16[512,1024]{1,0:T(8,128)(2,1)} collective-permute-done((bf16[512,1024]{1,0:T(8,128)(2,1)S(1)}, bf16[512,1024]{1,0:T(8,128)(2,1)}, u32[]{:S(2)}, u32[]{:S(2)}) %collective-permute-start.8) | collective-permute-done | bytes 1048608 | tf_op jit(solution)/shard_map/ppermute | solution.py:345
  148.9 6.2 place.9
  161.1 7.9 multiply_convert_fusion.6
  175.3 5.9 fusion.190
  182.5 12.2 %collective-permute-done.35.refs_1_ = bf16[512,1024]{1,0:T(8,128)(2,1)} collective-permute-done((bf16[512,1024]{1,0:T(8,128)(2,1)}, bf16[512,1024]{1,0:T(8,128)(2,1)}, u32[]{:S(2)}, u32[]{:S(2)}) %collective-permute-start.35) | collective-permute-done | bytes 1048608 | tf_op jit(solution)/shard_map/ppermute | solution.py:345
  195.8 8.8 place.8
  204.6 8.1 fusion.2.joined
  216.5 14.8 %attend_forward.1 = (bf16[512,1024]{1,0:T(8,128)(2,1)}, bf16[2,8,256,256]{3,2,1,0:T(8,128)(2,1)}) custom-call(s32[2]{0:T(128)} %lengths.1, f32[512,3072]{1,0:T(8,128)} %fusion.2.joined, f32[2,1024]{1,0:T(2,128)} %slice.172.biases, bf16[512,1024]{1,0:T(8,128)(2,1)} %fusion.139.relative), custom_call_target="tpu_custom_call" | custom-call | flops 1342177280 | bytes 8388608 | tf_op jit(solution)/shard_map/attend_forward/pallas_call | solution.py:157
  235.6 4.9 fusion.6
  269.7 4.4 place.11
  280.4 4.8 multiply_convert_fusion.5
  289.8 4.7 multiply_convert_fusion.4
  304.0 6.4 multiply_convert_fusion.3
  310.4 5.2 multiply_convert_fusion.2
  315.6 5.0 fusion.113
  320.7 5.4 fusion.110
  344.9 5.0 multiply_reduce_fusion.12
  367.0 4.8 multiply_reduce_fusion.3
  384.2 28.4 %collective-permute-done.118 = bf16[1024,1024]{1,0:T(8,128)(2,1)S(1)} collective-permute-done((bf16[1024,1024]{1,0:T(8,128)(2,1)}, bf16[1024,1024]{1,0:T(8,128)(2,1)S(1)}, u32[]{:S(2)}, u32[]{:S(2)}) %collective-permute-start.118) | collective-permute-done | bytes 2097184 | tf_op jit(solution)/shard_map/ppermute | solution.py:345
  427.1 19.7 %attend_backward.1 = (bf16[512,3072]{1,0:T(8,128)(2,1)}, f32[512,1024]{1,0:T(8,128)}, f32[2,1024]{1,0:T(2,128)}) custom-call(f32[512,3072]{1,0:T(8,128)} %fusion.2.joined, f32[2,1024]{1,0:T(2,128)} %slice.172.biases, bf16[512,1024]{1,0:T(8,128)(2,1)} %fusion.139.relative, bf16[2,8,256,256]{3,2,1,0:T(8,128)(2,1)} %get-tuple-element.57.probs, ...), custom_call_target="tpu_custom_call" | custom-call | flops 3221225472 | bytes 12582912 | tf_op jit(solution)/shard_map/attend_backward/pallas_call | solution.py:189
  462.2 6.7 collective-permute-done.120
  472.6 5.1 convolution_convert_fusion
  479.4 8.2 multiply_reduce_fusion.9
  488.4 6.6 multiply_convert_fusion.1
  495.0 5.2 multiply_convert_fusion
  510.8 10.8 %collective-permute-done.122 = bf16[128,1024]{1,0:T(8,128)(2,1)S(1)} collective-permute-done((bf16[128,1024]{1,0:T(8,128)(2,1)S(1)}, bf16[128,1024]{1,0:T(8,128)(2,1)S(1)}, u32[]{:S(2)}, u32[]{:S(2)}) %collective-permute-start.122) | collective-permute-done | bytes 262176 | tf_op jit(solution)/shard_map/ppermute | solution.py:351
  521.7 4.3 collective-permute-done.101
  528.2 11.4 %collective-permute-done.111 = bf16[256,1024]{1,0:T(8,128)(2,1)S(1)} collective-permute-done((bf16[256,1024]{1,0:T(8,128)(2,1)S(1)}, bf16[256,1024]{1,0:T(8,128)(2,1)S(1)}, u32[]{:S(2)}, u32[]{:S(2)}) %collective-permute-start.111) | collective-permute-done | bytes 524320 | tf_op jit(solution)/shard_map/ppermute | solution.py:348
  542.2 4.9 fusion.96
  547.1 9.4 collective-permute-done.102
  564.0 19.2 %collective-permute-done.103 = bf16[64,1536]{1,0:T(8,128)(2,1)S(1)} collective-permute-done((bf16[64,1536]{1,0:T(8,128)(2,1)S(1)}, bf16[64,1536]{1,0:T(8,128)(2,1)S(1)}, u32[]{:S(2)}, u32[]{:S(2)}) %collective-permute-start.103) | collective-permute-done | bytes 196640 | tf_op jit(solution)/shard_map/ppermute | solution.py:351
  587.6 5.6 collective-permute-done.104
  599.4 6.2 collective-permute-done.105
  607.1 5.6 fusion.90
  612.6 5.7 fusion.87
  625.1 4.3 fusion.23
  633.5 20.9 %collective-permute-done.82 = bf16[1024,1024]{1,0:T(8,128)(2,1)} collective-permute-done((bf16[1024,1024]{1,0:T(8,128)(2,1)}, bf16[1024,1024]{1,0:T(8,128)(2,1)}, u32[]{:S(2)}, u32[]{:S(2)}) %collective-permute-start.82) | collective-permute-done | bytes 2097184 | tf_op jit(solution)/shard_map/ppermute | solution.py:345
  661.1 36.9 %collective-permute-done.69 = f32[12,1024]{1,0:T(8,128)S(1)} collective-permute-done((f32[12,1024]{1,0:T(8,128)S(1)}, f32[12,1024]{1,0:T(8,128)S(1)}, u32[]{:S(2)}, u32[]{:S(2)}) %collective-permute-start.69) | collective-permute-done | bytes 49184 | tf_op jit(solution)/shard_map/ppermute | solution.py:357
  705.2 9.9 %collective-permute-done.93 = bf16[128,2560]{1,0:T(8,128)(2,1)S(1)} collective-permute-done((bf16[128,2560]{1,0:T(8,128)(2,1)S(1)}, bf16[128,2560]{1,0:T(8,128)(2,1)S(1)}, u32[]{:S(2)}, u32[]{:S(2)}) %collective-permute-start.93) | collective-permute-done | bytes 655392 | tf_op jit(solution)/shard_map/ppermute | solution.py:348
  716.5 12.1 %collective-permute-done.84 = bf16[256,1024]{1,0:T(8,128)(2,1)S(1)} collective-permute-done((bf16[256,1024]{1,0:T(8,128)(2,1)S(1)}, bf16[256,1024]{1,0:T(8,128)(2,1)S(1)}, u32[]{:S(2)}, u32[]{:S(2)}) %collective-permute-start.84) | collective-permute-done | bytes 524320 | tf_op jit(solution)/shard_map/ppermute | solution.py:348
  732.7 13.4 %collective-permute-done.94 = bf16[64,2560]{1,0:T(8,128)(2,1)S(1)} collective-permute-done((bf16[64,2560]{1,0:T(8,128)(2,1)S(1)}, bf16[64,2560]{1,0:T(8,128)(2,1)S(1)}, u32[]{:S(2)}, u32[]{:S(2)}) %collective-permute-start.94) | collective-permute-done | bytes 327712 | tf_op jit(solution)/shard_map/ppermute | solution.py:351
  746.2 12.8 %collective-permute-done.75 = bf16[256,1024]{1,0:T(8,128)(2,1)S(1)} collective-permute-done((bf16[256,1024]{1,0:T(8,128)(2,1)S(1)}, bf16[256,1024]{1,0:T(8,128)(2,1)S(1)}, u32[]{:S(2)}, u32[]{:S(2)}) %collective-permute-start.75) | collective-permute-done | bytes 524320 | tf_op jit(solution)/shard_map/ppermute | solution.py:348
  765.3 12.3 %collective-permute-done.70 = f32[12,1024]{1,0:T(8,128)S(1)} collective-permute-done((f32[12,1024]{1,0:T(8,128)S(1)}, f32[12,1024]{1,0:T(8,128)S(1)}, u32[]{:S(2)}, u32[]{:S(2)}) %collective-permute-start.70) | collective-permute-done | bytes 49184 | tf_op jit(solution)/shard_map/ppermute | solution.py:360
  780.5 18.5 %collective-permute-done.85 = bf16[128,1024]{1,0:T(8,128)(2,1)S(1)} collective-permute-done((bf16[128,1024]{1,0:T(8,128)(2,1)S(1)}, bf16[128,1024]{1,0:T(8,128)(2,1)S(1)}, u32[]{:S(2)}, u32[]{:S(2)}) %collective-permute-start.85) | collective-permute-done | bytes 262176 | tf_op jit(solution)/shard_map/ppermute | solution.py:351
  806.7 11.4 %collective-permute-done.86 = bf16[128,1024]{1,0:T(8,128)(2,1)S(1)} collective-permute-done((bf16[128,1024]{1,0:T(8,128)(2,1)S(1)}, bf16[128,1024]{1,0:T(8,128)(2,1)S(1)}, u32[]{:S(2)}, u32[]{:S(2)}) %collective-permute-start.86) | collective-permute-done | bytes 262176 | tf_op jit(solution)/shard_map/ppermute | solution.py:351
  818.1 8.8 collective-permute-done.77
  830.3 11.5 %collective-permute-done.87 = bf16[256,1024]{1,0:T(8,128)(2,1)S(1)} collective-permute-done((bf16[256,1024]{1,0:T(8,128)(2,1)S(1)}, bf16[256,1024]{1,0:T(8,128)(2,1)S(1)}, u32[]{:S(2)}, u32[]{:S(2)}) %collective-permute-start.87) | collective-permute-done | bytes 524320 | tf_op jit(solution)/shard_map/ppermute | solution.py:348
  841.8 5.4 collective-permute-start.97
  852.4 6.0 collective-permute-start.88
  861.5 15.7 %collective-permute-done.97.refs_1_ = bf16[256,2560]{1,0:T(8,128)(2,1)} collective-permute-done((bf16[256,2560]{1,0:T(8,128)(2,1)}, bf16[256,2560]{1,0:T(8,128)(2,1)}, u32[]{:S(2)}, u32[]{:S(2)}) %collective-permute-start.97) | collective-permute-done | bytes 1310752 | tf_op jit(solution)/shard_map/ppermute | solution.py:345
  877.2 22.5 %collective-permute-done.88.refs_1_ = bf16[512,1024]{1,0:T(8,128)(2,1)} collective-permute-done((bf16[512,1024]{1,0:T(8,128)(2,1)}, bf16[512,1024]{1,0:T(8,128)(2,1)}, u32[]{:S(2)}, u32[]{:S(2)}) %collective-permute-start.88) | collective-permute-done | bytes 1048608 | tf_op jit(solution)/shard_map/ppermute | solution.py:345
  900.2 17.2 %collective-permute-done.79.refs_1_ = bf16[512,1024]{1,0:T(8,128)(2,1)} collective-permute-done((bf16[512,1024]{1,0:T(8,128)(2,1)}, bf16[512,1024]{1,0:T(8,128)(2,1)}, u32[]{:S(2)}, u32[]{:S(2)}) %collective-permute-start.79) | collective-permute-done | bytes 1048608 | tf_op jit(solution)/shard_map/ppermute | solution.py:345
  922.0 5.4 widen.11
  927.4 4.8 widen.9
  932.2 5.4 widen.10
  937.6 5.4 widen.7
  945.1 6.4 widen.8
  953.5 5.4 widen.6
  (668 shorter events, 333.0 us)
Async XLA Ops:
  8.7 34.0 %collective-permute-start = (bf16[14,512]{1,0:T(8,128)(2,1)}, bf16[14,512]{1,0:T(8,128)(2,1)}, u32[]{:S(2)}, u32[]{:S(2)}) collective-permute-start(bf16[14,512]{1,0:T(8,128)(2,1)} %concatenate.154), channel_id=1, source_target_pairs={{0,1},{1,0},{2,3},{3,2},{4,5},{5,4},{6,7},{7,6},{8,9},{9,8},{10,11... | collective-permute-start | bytes 43016 | tf_op jit(solution)/shard_map/ppermute | solution.py:345
  13.6 40.1 %collective-permute-start.1 = (bf16[128,2048]{1,0:T(8,128)(2,1)}, bf16[128,2048]{1,0:T(8,128)(2,1)}, u32[]{:S(2)}, u32[]{:S(2)}) collective-permute-start(bf16[128,2048]{1,0:T(8,128)(2,1)} %constant_dynamic-slice_fusion.30), channel_id=1, source_target_pairs={{0,1},{1,0},{2,3},{3,2},{4,5},{5,4},{6,7},{7,6},{8,9},{9,8},{10,11... | collective-permute-start | bytes 1572872 | tf_op jit(solution)/shard_map/ppermute | solution.py:345
  15.4 52.4 %collective-permute-start.6 = (bf16[256,1024]{1,0:T(8,128)(2,1)}, bf16[256,1024]{1,0:T(8,128)(2,1)}, u32[]{:S(2)}, u32[]{:S(2)}) collective-permute-start(bf16[256,1024]{1,0:T(8,128)(2,1)} %constant_dynamic-slice_fusion.29), channel_id=1, source_target_pairs={{0,1},{1,0},{2,3},{3,2},{4,5},{5,4},{6,7},{7,6},{8,9},{9,8},{10,11... | collective-permute-start | bytes 1572872 | tf_op jit(solution)/shard_map/ppermute | solution.py:345
  25.8 49.4 %collective-permute-start.11 = (bf16[64,5120]{1,0:T(8,128)(2,1)}, bf16[64,5120]{1,0:T(8,128)(2,1)}, u32[]{:S(2)}, u32[]{:S(2)}) collective-permute-start(bf16[64,5120]{1,0:T(8,128)(2,1)} %constant_dynamic-slice_fusion.28), channel_id=1, source_target_pairs={{0,1},{1,0},{2,3},{3,2},{4,5},{5,4},{6,7},{7,6},{8,9},{9,8},{10,11... | collective-permute-start | bytes 1966088 | tf_op jit(solution)/shard_map/ppermute | solution.py:345
  27.2 35.1 %collective-permute-start.16 = (bf16[64,3072]{1,0:T(8,128)(2,1)S(1)}, bf16[64,3072]{1,0:T(8,128)(2,1)S(1)}, u32[]{:S(2)}, u32[]{:S(2)}) collective-permute-start(bf16[64,3072]{1,0:T(8,128)(2,1)S(1)} %constant_dynamic-slice_fusion.27), channel_id=1, source_target_pairs={{0,1},{1,0},{2,3},{3,2},{4,5},{5,4},{6,7},{7,6},{8,9},{9,8},{10,11... | collective-permute-start | bytes 1179656 | tf_op jit(solution)/shard_map/ppermute | solution.py:345
  42.7 30.8 %collective-permute-start.28 = (bf16[128,2048]{1,0:T(8,128)(2,1)S(1)}, bf16[128,2048]{1,0:T(8,128)(2,1)S(1)}, u32[]{:S(2)}, u32[]{:S(2)}) collective-permute-start(bf16[128,2048]{1,0:T(8,128)(2,1)S(1)} %constant_dynamic-slice_fusion.26), channel_id=1, source_target_pairs={{0,1},{1,0},{2,3},{3,2},{4,5},{5,4},{6,7},{7,6},{8,9},{9,8},{10,11... | collective-permute-start | bytes 1572872 | tf_op jit(solution)/shard_map/ppermute | solution.py:345
  67.9 53.4 %collective-permute-start.3 = (bf16[256,2048]{1,0:T(8,128)(2,1)S(1)}, bf16[256,2048]{1,0:T(8,128)(2,1)S(1)}, u32[]{:S(2)}, u32[]{:S(2)}) collective-permute-start(bf16[256,2048]{1,0:T(8,128)(2,1)S(1)} %constant_dynamic-update-slice_fusion.refs_0_), channel_id=1, source_target_pairs={{0,8},{8,0},{16,24},{24,16},{1,9},{9,1},{17,25},{25,17},{2,10},{10... | collective-permute-start | bytes 3145736 | tf_op jit(solution)/shard_map/ppermute | solution.py:348
  73.6 38.4 %collective-permute-start.7 = (bf16[256,1024]{1,0:T(8,128)(2,1)}, bf16[256,1024]{1,0:T(8,128)(2,1)S(1)}, u32[]{:S(2)}, u32[]{:S(2)}) collective-permute-start(bf16[256,1024]{1,0:T(8,128)(2,1)} %collective-permute-done.6), channel_id=1, source_target_pairs={{0,8},{8,0},{16,24},{24,16},{1,9},{9,1},{17,25},{25,17},{2,10},{10... | collective-permute-start | bytes 1572872 | tf_op jit(solution)/shard_map/ppermute | solution.py:348
  75.2 44.5 %collective-permute-start.12 = (bf16[64,5120]{1,0:T(8,128)(2,1)}, bf16[64,5120]{1,0:T(8,128)(2,1)S(1)}, u32[]{:S(2)}, u32[]{:S(2)}) collective-permute-start(bf16[64,5120]{1,0:T(8,128)(2,1)} %collective-permute-done.11), channel_id=1, source_target_pairs={{0,4},{4,0},{1,5},{5,1},{2,6},{6,2},{3,7},{7,3},{8,12},{12,8},{9,1... | collective-permute-start | bytes 1966088 | tf_op jit(solution)/shard_map/ppermute | solution.py:345
  83.3 31.1 %collective-permute-start.29 = (bf16[128,2048]{1,0:T(8,128)(2,1)S(1)}, bf16[128,2048]{1,0:T(8,128)(2,1)S(1)}, u32[]{:S(2)}, u32[]{:S(2)}) collective-permute-start(bf16[128,2048]{1,0:T(8,128)(2,1)S(1)} %collective-permute-done.28), channel_id=1, source_target_pairs={{0,4},{4,0},{1,5},{5,1},{2,6},{6,2},{3,7},{7,3},{8,12},{12,8},{9,1... | collective-permute-start | bytes 1572872 | tf_op jit(solution)/shard_map/ppermute | solution.py:345
  84.9 34.9 %collective-permute-start.34 = (bf16[256,1024]{1,0:T(8,128)(2,1)S(1)}, bf16[256,1024]{1,0:T(8,128)(2,1)S(1)}, u32[]{:S(2)}, u32[]{:S(2)}) collective-permute-start(bf16[256,1024]{1,0:T(8,128)(2,1)S(1)} %collective-permute-done.33), channel_id=1, source_target_pairs={{0,8},{8,0},{16,24},{24,16},{1,9},{9,1},{17,25},{25,17},{2,10},{10... | collective-permute-start | bytes 1572872 | tf_op jit(solution)/shard_map/ppermute | solution.py:348
  119.7 35.3 %collective-permute-start.4 = (bf16[256,2048]{1,0:T(8,128)(2,1)S(1)}, bf16[256,2048]{1,0:T(8,128)(2,1)}, u32[]{:S(2)}, u32[]{:S(2)}) collective-permute-start(bf16[256,2048]{1,0:T(8,128)(2,1)S(1)} %constant_dynamic-update-slice_fusion.refs_0_), channel_id=1, source_target_pairs={{0,2},{2,0},{1,3},{3,1},{4,6},{6,4},{5,7},{7,5},{8,10},{10,8},{9,1... | collective-permute-start | bytes 3145736 | tf_op jit(solution)/shard_map/ppermute | solution.py:345
  121.3 35.3 %collective-permute-start.5 = (bf16[256,2048]{1,0:T(8,128)(2,1)S(1)}, bf16[256,2048]{1,0:T(8,128)(2,1)}, u32[]{:S(2)}, u32[]{:S(2)}) collective-permute-start(bf16[256,2048]{1,0:T(8,128)(2,1)S(1)} %collective-permute-done.3.refs_1_), channel_id=1, source_target_pairs={{0,2},{2,0},{1,3},{3,1},{4,6},{6,4},{5,7},{7,5},{8,10},{10,8},{9,1... | collective-permute-start | bytes 3145736 | tf_op jit(solution)/shard_map/ppermute | solution.py:345
  126.3 44.3 %collective-permute-start.13 = (bf16[128,5120]{1,0:T(8,128)(2,1)S(1)}, bf16[128,5120]{1,0:T(8,128)(2,1)}, u32[]{:S(2)}, u32[]{:S(2)}) collective-permute-start(bf16[128,5120]{1,0:T(8,128)(2,1)S(1)} %constant_dynamic-update-slice_fusion.7.refs_0_), channel_id=1, source_target_pairs={{0,8},{8,0},{16,24},{24,16},{1,9},{9,1},{17,25},{25,17},{2,10},{10... | collective-permute-start | bytes 3932168 | tf_op jit(solution)/shard_map/ppermute | solution.py:348
  155.0 27.4 %collective-permute-start.30 = (bf16[256,2048]{1,0:T(8,128)(2,1)S(1)}, bf16[256,2048]{1,0:T(8,128)(2,1)}, u32[]{:S(2)}, u32[]{:S(2)}) collective-permute-start(bf16[256,2048]{1,0:T(8,128)(2,1)S(1)} %constant_dynamic-update-slice_fusion.13.refs_0_), channel_id=1, source_target_pairs={{0,8},{8,0},{16,24},{24,16},{1,9},{9,1},{17,25},{25,17},{2,10},{10... | collective-permute-start | bytes 3145736 | tf_op jit(solution)/shard_map/ppermute | solution.py:348
  156.7 104.4 %collective-permute-start.31 = (bf16[256,2048]{1,0:T(8,128)(2,1)S(1)}, bf16[256,2048]{1,0:T(8,128)(2,1)}, u32[]{:S(2)}, u32[]{:S(2)}) collective-permute-start(bf16[256,2048]{1,0:T(8,128)(2,1)S(1)} %constant_dynamic-update-slice_fusion.13.refs_0_), channel_id=1, source_target_pairs={{0,2},{2,0},{1,3},{3,1},{4,6},{6,4},{5,7},{7,5},{8,10},{10,8},{9,1... | collective-permute-start | bytes 3145736 | tf_op jit(solution)/shard_map/ppermute | solution.py:345
  182.4 87.2 %collective-permute-start.36 = (bf16[512,1024]{1,0:T(8,128)(2,1)}, bf16[512,1024]{1,0:T(8,128)(2,1)}, u32[]{:S(2)}, u32[]{:S(2)}) collective-permute-start(bf16[512,1024]{1,0:T(8,128)(2,1)} %constant_dynamic-update-slice_fusion.15.refs_0_), channel_id=1, source_target_pairs={{0,2},{2,0},{1,3},{3,1},{4,6},{6,4},{5,7},{7,5},{8,10},{10,8},{9,1... | collective-permute-start | bytes 3145736 | tf_op jit(solution)/shard_map/ppermute | solution.py:345
  194.7 69.9 %collective-permute-start.32 = (bf16[256,2048]{1,0:T(8,128)(2,1)}, bf16[256,2048]{1,0:T(8,128)(2,1)}, u32[]{:S(2)}, u32[]{:S(2)}) collective-permute-start(bf16[256,2048]{1,0:T(8,128)(2,1)} %collective-permute-done.30.refs_1_), channel_id=1, source_target_pairs={{0,2},{2,0},{1,3},{3,1},{4,6},{6,4},{5,7},{7,5},{8,10},{10,8},{9,1... | collective-permute-start | bytes 3145736 | tf_op jit(solution)/shard_map/ppermute | solution.py:345
  194.7 75.0 %collective-permute-start.37 = (bf16[512,1024]{1,0:T(8,128)(2,1)}, bf16[512,1024]{1,0:T(8,128)(2,1)}, u32[]{:S(2)}, u32[]{:S(2)}) collective-permute-start(bf16[512,1024]{1,0:T(8,128)(2,1)} %collective-permute-done.35.refs_1_), channel_id=1, source_target_pairs={{0,2},{2,0},{1,3},{3,1},{4,6},{6,4},{5,7},{7,5},{8,10},{10,8},{9,1... | collective-permute-start | bytes 3145736 | tf_op jit(solution)/shard_map/ppermute | solution.py:345
  285.3 41.8 %collective-permute-start.38 = (bf16[512,1024]{1,0:T(8,128)(2,1)S(1)}, bf16[512,1024]{1,0:T(8,128)(2,1)S(1)}, u32[]{:S(2)}, u32[]{:S(2)}) collective-permute-start(bf16[512,1024]{1,0:T(8,128)(2,1)S(1)} %multiply_convert_fusion.13), channel_id=1, source_target_pairs={{0,2},{2,0},{1,3},{3,1},{4,6},{6,4},{5,7},{7,5},{8,10},{10,8},{9,1... | collective-permute-start | bytes 3145736 | tf_op jit(solution)/shard_map/ppermute | solution.py:345
  287.9 27.7 %collective-permute-start.39 = (bf16[512,1024]{1,0:T(8,128)(2,1)S(1)}, bf16[512,1024]{1,0:T(8,128)(2,1)S(1)}, u32[]{:S(2)}, u32[]{:S(2)}) collective-permute-start(bf16[512,1024]{1,0:T(8,128)(2,1)S(1)} %get-tuple-element.143), channel_id=1, source_target_pairs={{0,2},{2,0},{1,3},{3,1},{4,6},{6,4},{5,7},{7,5},{8,10},{10,8},{9,1... | collective-permute-start | bytes 3145736 | tf_op jit(solution)/shard_map/ppermute | solution.py:345
  362.7 51.9 %collective-permute-start.44 = (bf16[512,1024]{1,0:T(8,128)(2,1)}, bf16[512,1024]{1,0:T(8,128)(2,1)S(1)}, u32[]{:S(2)}, u32[]{:S(2)}) collective-permute-start(bf16[512,1024]{1,0:T(8,128)(2,1)} %copy-done.52), channel_id=1, source_target_pairs={{0,2},{2,0},{1,3},{3,1},{4,6},{6,4},{5,7},{7,5},{8,10},{10,8},{9,1... | collective-permute-start | bytes 3145736 | tf_op jit(solution)/shard_map/ppermute | solution.py:345
  363.8 48.8 %collective-permute-start.118 = (bf16[1024,1024]{1,0:T(8,128)(2,1)}, bf16[1024,1024]{1,0:T(8,128)(2,1)S(1)}, u32[]{:S(2)}, u32[]{:S(2)}) collective-permute-start(bf16[1024,1024]{1,0:T(8,128)(2,1)} %fusion.110), channel_id=1, source_target_pairs={{0,1},{1,0},{2,3},{3,2},{4,5},{5,4},{6,7},{7,6},{8,9},{9,8},{10,11... | collective-permute-start | bytes 6291464 | tf_op jit(solution)/shard_map/ppermute | solution.py:345
  377.0 37.6 %collective-permute-start.52 = (bf16[512,1024]{1,0:T(8,128)(2,1)S(1)}, bf16[512,1024]{1,0:T(8,128)(2,1)S(1)}, u32[]{:S(2)}, u32[]{:S(2)}) collective-permute-start(bf16[512,1024]{1,0:T(8,128)(2,1)S(1)} %get-tuple-element.131), channel_id=1, source_target_pairs={{0,2},{2,0},{1,3},{3,1},{4,6},{6,4},{5,7},{7,5},{8,10},{10,8},{9,1... | collective-permute-start | bytes 3145736 | tf_op jit(solution)/shard_map/ppermute | solution.py:345
  381.8 72.6 %collective-permute-start.58 = (bf16[512,1024]{1,0:T(8,128)(2,1)}, bf16[512,1024]{1,0:T(8,128)(2,1)}, u32[]{:S(2)}, u32[]{:S(2)}) collective-permute-start(bf16[512,1024]{1,0:T(8,128)(2,1)} %get-tuple-element.51), channel_id=1, source_target_pairs={{0,2},{2,0},{1,3},{3,1},{4,6},{6,4},{5,7},{7,5},{8,10},{10,8},{9,1... | collective-permute-start | bytes 3145736 | tf_op jit(solution)/shard_map/ppermute | solution.py:345
  381.9 77.1 %collective-permute-start.109 = (bf16[1024,1024]{1,0:T(8,128)(2,1)}, bf16[1024,1024]{1,0:T(8,128)(2,1)}, u32[]{:S(2)}, u32[]{:S(2)}) collective-permute-start(bf16[1024,1024]{1,0:T(8,128)(2,1)} %fusion.104), channel_id=1, source_target_pairs={{0,1},{1,0},{2,3},{3,2},{4,5},{5,4},{6,7},{7,6},{8,9},{9,8},{10,11... | collective-permute-start | bytes 6291464 | tf_op jit(solution)/shard_map/ppermute | solution.py:345
  413.0 38.4 %collective-permute-start.119 = (bf16[512,1024]{1,0:T(8,128)(2,1)S(1)}, bf16[512,1024]{1,0:T(8,128)(2,1)}, u32[]{:S(2)}, u32[]{:S(2)}) collective-permute-start(bf16[512,1024]{1,0:T(8,128)(2,1)S(1)} %add_convert_fusion.1), channel_id=1, source_target_pairs={{0,4},{4,0},{1,5},{5,1},{2,6},{6,2},{3,7},{7,3},{8,12},{12,8},{9,1... | collective-permute-start | bytes 3145736 | tf_op jit(solution)/shard_map/ppermute | solution.py:345
  427.0 28.0 %collective-permute-start.59 = (bf16[512,512]{1,0:T(8,128)(2,1)S(1)}, bf16[512,512]{1,0:T(8,128)(2,1)S(1)}, u32[]{:S(2)}, u32[]{:S(2)}) collective-permute-start(bf16[512,512]{1,0:T(8,128)(2,1)S(1)} %get-tuple-element.149), channel_id=1, source_target_pairs={{0,2},{2,0},{1,3},{3,1},{4,6},{6,4},{5,7},{7,5},{8,10},{10,8},{9,1... | collective-permute-start | bytes 1572872 | tf_op jit(solution)/shard_map/ppermute | solution.py:345
  458.1 148.7 %collective-permute-start.60 = (bf16[512,1024]{1,0:T(8,128)(2,1)}, bf16[512,1024]{1,0:T(8,128)(2,1)}, u32[]{:S(2)}, u32[]{:S(2)}) collective-permute-start(bf16[512,1024]{1,0:T(8,128)(2,1)} %fusion.17), channel_id=1, source_target_pairs={{0,2},{2,0},{1,3},{3,1},{4,6},{6,4},{5,7},{7,5},{8,10},{10,8},{9,1... | collective-permute-start | bytes 3145736 | tf_op jit(solution)/shard_map/ppermute | solution.py:345
  458.9 81.4 %collective-permute-start.61 = (bf16[512,1024]{1,0:T(8,128)(2,1)}, bf16[512,1024]{1,0:T(8,128)(2,1)}, u32[]{:S(2)}, u32[]{:S(2)}) collective-permute-start(bf16[512,1024]{1,0:T(8,128)(2,1)} %get-tuple-element.129), channel_id=1, source_target_pairs={{0,2},{2,0},{1,3},{3,1},{4,6},{6,4},{5,7},{7,5},{8,10},{10,8},{9,1... | collective-permute-start | bytes 3145736 | tf_op jit(solution)/shard_map/ppermute | solution.py:345
  469.0 35.6 %collective-permute-start.100 = (bf16[512,1536]{1,0:T(8,128)(2,1)S(1)}, bf16[512,1536]{1,0:T(8,128)(2,1)}, u32[]{:S(2)}, u32[]{:S(2)}) collective-permute-start(bf16[512,1536]{1,0:T(8,128)(2,1)S(1)} %constant_dynamic-slice_fusion), channel_id=1, source_target_pairs={{0,1},{1,0},{2,3},{3,2},{4,5},{5,4},{6,7},{7,6},{8,9},{9,8},{10,11... | collective-permute-start | bytes 4718600 | tf_op jit(solution)/shard_map/ppermute | solution.py:345
  469.2 37.4 %collective-permute-start.110 = (bf16[512,1024]{1,0:T(8,128)(2,1)}, bf16[512,1024]{1,0:T(8,128)(2,1)}, u32[]{:S(2)}, u32[]{:S(2)}) collective-permute-start(bf16[512,1024]{1,0:T(8,128)(2,1)} %add_convert_fusion.2), channel_id=1, source_target_pairs={{0,4},{4,0},{1,5},{5,1},{2,6},{6,2},{3,7},{7,3},{8,12},{12,8},{9,1... | collective-permute-start | bytes 3145736 | tf_op jit(solution)/shard_map/ppermute | solution.py:345
  470.7 35.3 %collective-permute-start.121 = (bf16[128,1024]{1,0:T(8,128)(2,1)S(1)}, bf16[128,1024]{1,0:T(8,128)(2,1)S(1)}, u32[]{:S(2)}, u32[]{:S(2)}) collective-permute-start(bf16[128,1024]{1,0:T(8,128)(2,1)S(1)} %dynamic-slice_convert_fusion.7), channel_id=1, source_target_pairs={{0,16},{16,0},{8,24},{24,8},{1,17},{17,1},{9,25},{25,9},{2,18},{18... | collective-permute-start | bytes 786440 | tf_op jit(solution)/shard_map/ppermute | solution.py:351
  504.6 52.1 %collective-permute-start.63 = (bf16[512,1024]{1,0:T(8,128)(2,1)S(1)}, bf16[512,1024]{1,0:T(8,128)(2,1)S(1)}, u32[]{:S(2)}, u32[]{:S(2)}) collective-permute-start(bf16[512,1024]{1,0:T(8,128)(2,1)S(1)} %copy-done.59), channel_id=1, source_target_pairs={{0,2},{2,0},{1,3},{3,1},{4,6},{6,4},{5,7},{7,5},{8,10},{10,8},{9,1... | collective-permute-start | bytes 3145736 | tf_op jit(solution)/shard_map/ppermute | solution.py:345
  540.4 78.0 %collective-permute-start.91 = (bf16[512,2560]{1,0:T(8,128)(2,1)S(1)}, bf16[512,2560]{1,0:T(8,128)(2,1)S(1)}, u32[]{:S(2)}, u32[]{:S(2)}) collective-permute-start(bf16[512,2560]{1,0:T(8,128)(2,1)S(1)} %constant_dynamic-slice_fusion.1), channel_id=1, source_target_pairs={{0,1},{1,0},{2,3},{3,2},{4,5},{5,4},{6,7},{7,6},{8,9},{9,8},{10,11... | collective-permute-start | bytes 7864328 | tf_op jit(solution)/shard_map/ppermute | solution.py:345
  540.7 52.4 %collective-permute-start.123 = (bf16[256,1024]{1,0:T(8,128)(2,1)S(1)}, bf16[256,1024]{1,0:T(8,128)(2,1)S(1)}, u32[]{:S(2)}, u32[]{:S(2)}) collective-permute-start(bf16[256,1024]{1,0:T(8,128)(2,1)S(1)} %pad_maximum_fusion.28), channel_id=1, source_target_pairs={{0,8},{8,0},{16,24},{24,16},{1,9},{9,1},{17,25},{25,17},{2,10},{10... | collective-permute-start | bytes 1572872 | tf_op jit(solution)/shard_map/ppermute | solution.py:348
  605.5 48.9 %collective-permute-start.82 = (bf16[1024,1024]{1,0:T(8,128)(2,1)}, bf16[1024,1024]{1,0:T(8,128)(2,1)}, u32[]{:S(2)}, u32[]{:S(2)}) collective-permute-start(bf16[1024,1024]{1,0:T(8,128)(2,1)} %fusion.93), channel_id=1, source_target_pairs={{0,1},{1,0},{2,3},{3,2},{4,5},{5,4},{6,7},{7,6},{8,9},{9,8},{10,11... | collective-permute-start | bytes 6291464 | tf_op jit(solution)/shard_map/ppermute | solution.py:345
  620.3 36.0 %collective-permute-start.92 = (bf16[256,2560]{1,0:T(8,128)(2,1)}, bf16[256,2560]{1,0:T(8,128)(2,1)}, u32[]{:S(2)}, u32[]{:S(2)}) collective-permute-start(bf16[256,2560]{1,0:T(8,128)(2,1)} %add_convert_fusion), channel_id=1, source_target_pairs={{0,4},{4,0},{1,5},{5,1},{2,6},{6,2},{3,7},{7,3},{8,12},{12,8},{9,1... | collective-permute-start | bytes 3932168 | tf_op jit(solution)/shard_map/ppermute | solution.py:345
  624.0 75.3 %collective-permute-start.73 = (bf16[1024,1024]{1,0:T(8,128)(2,1)}, bf16[1024,1024]{1,0:T(8,128)(2,1)}, u32[]{:S(2)}, u32[]{:S(2)}) collective-permute-start(bf16[1024,1024]{1,0:T(8,128)(2,1)} %fusion.87), channel_id=1, source_target_pairs={{0,1},{1,0},{2,3},{3,2},{4,5},{5,4},{6,7},{7,6},{8,9},{9,8},{10,11... | collective-permute-start | bytes 6291464 | tf_op jit(solution)/shard_map/ppermute | solution.py:345
  631.0 29.2 %collective-permute-start.68 = (f32[12,1024]{1,0:T(8,128)S(1)}, f32[12,1024]{1,0:T(8,128)S(1)}, u32[]{:S(2)}, u32[]{:S(2)}) collective-permute-start(f32[12,1024]{1,0:T(8,128)S(1)} %add.503), channel_id=1, source_target_pairs={{0,4},{4,0},{1,5},{5,1},{2,6},{6,2},{3,7},{7,3},{8,12},{12,8},{9,1... | collective-permute-start | bytes 147464 | tf_op jit(solution)/shard_map/ppermute | solution.py:345
  632.6 65.3 %collective-permute-start.69 = (f32[12,1024]{1,0:T(8,128)S(1)}, f32[12,1024]{1,0:T(8,128)S(1)}, u32[]{:S(2)}, u32[]{:S(2)}) collective-permute-start(f32[12,1024]{1,0:T(8,128)S(1)} %add.503), channel_id=1, source_target_pairs={{0,5},{5,0},{1,4},{4,1},{2,7},{7,2},{3,6},{6,3},{8,13},{13,8},{9,1... | collective-permute-start | bytes 147464 | tf_op jit(solution)/shard_map/ppermute | solution.py:357
  654.4 44.2 %collective-permute-start.67 = (f32[12,1024]{1,0:T(8,128)S(1)}, f32[12,1024]{1,0:T(8,128)S(1)}, u32[]{:S(2)}, u32[]{:S(2)}) collective-permute-start(f32[12,1024]{1,0:T(8,128)S(1)} %add.503), channel_id=1, source_target_pairs={{0,1},{1,0},{2,3},{3,2},{4,5},{5,4},{6,7},{7,6},{8,9},{9,8},{10,11... | collective-permute-start | bytes 147464 | tf_op jit(solution)/shard_map/ppermute | solution.py:345
  656.3 46.0 %collective-permute-start.83 = (bf16[512,1024]{1,0:T(8,128)(2,1)S(1)}, bf16[512,1024]{1,0:T(8,128)(2,1)S(1)}, u32[]{:S(2)}, u32[]{:S(2)}) collective-permute-start(bf16[512,1024]{1,0:T(8,128)(2,1)S(1)} %add_convert_fusion.3), channel_id=1, source_target_pairs={{0,4},{4,0},{1,5},{5,1},{2,6},{6,2},{3,7},{7,3},{8,12},{12,8},{9,1... | collective-permute-start | bytes 3145736 | tf_op jit(solution)/shard_map/ppermute | solution.py:345
  660.2 100.4 %collective-permute-start.124 = (bf16[512,1024]{1,0:T(8,128)(2,1)S(1)}, bf16[512,1024]{1,0:T(8,128)(2,1)S(1)}, u32[]{:S(2)}, u32[]{:S(2)}) collective-permute-start(bf16[512,1024]{1,0:T(8,128)(2,1)S(1)} %copy-done.20), channel_id=1, source_target_pairs={{0,4},{4,0},{1,5},{5,1},{2,6},{6,2},{3,7},{7,3},{8,12},{12,8},{9,1... | collective-permute-start | bytes 3145736 | tf_op jit(solution)/shard_map/ppermute | solution.py:345
  698.0 64.3 %collective-permute-start.125 = (bf16[512,1024]{1,0:T(8,128)(2,1)S(1)}, bf16[512,1024]{1,0:T(8,128)(2,1)S(1)}, u32[]{:S(2)}, u32[]{:S(2)}) collective-permute-start(bf16[512,1024]{1,0:T(8,128)(2,1)S(1)} %copy-done.20), channel_id=1, source_target_pairs={{0,2},{2,0},{1,3},{3,1},{4,6},{6,4},{5,7},{7,5},{8,10},{10,8},{9,1... | collective-permute-start | bytes 3145736 | tf_op jit(solution)/shard_map/ppermute | solution.py:345
  699.2 65.9 %collective-permute-start.71 = (f32[12,1024]{1,0:T(8,128)S(1)}, f32[12,1024]{1,0:T(8,128)S(1)}, u32[]{:S(2)}, u32[]{:S(2)}) collective-permute-start(f32[12,1024]{1,0:T(8,128)S(1)} %add_add_fusion.1), channel_id=1, source_target_pairs={{0,8},{8,16},{16,24},{24,0},{1,9},{9,17},{17,25},{25,1},{2,10},{10... | collective-permute-start | bytes 147464 | tf_op jit(solution)/shard_map/ppermute | solution.py:360
  702.4 28.3 %collective-permute-start.74 = (bf16[512,1024]{1,0:T(8,128)(2,1)S(1)}, bf16[512,1024]{1,0:T(8,128)(2,1)S(1)}, u32[]{:S(2)}, u32[]{:S(2)}) collective-permute-start(bf16[512,1024]{1,0:T(8,128)(2,1)S(1)} %add_convert_fusion.4), channel_id=1, source_target_pairs={{0,4},{4,0},{1,5},{5,1},{2,6},{6,2},{3,7},{7,3},{8,12},{12,8},{9,1... | collective-permute-start | bytes 3145736 | tf_op jit(solution)/shard_map/ppermute | solution.py:345
  728.6 36.5 %collective-permute-start.72 = (f32[12,1024]{1,0:T(8,128)S(1)}, f32[12,1024]{1,0:T(8,128)S(1)}, u32[]{:S(2)}, u32[]{:S(2)}) collective-permute-start(f32[12,1024]{1,0:T(8,128)S(1)} %add_add_fusion.1), channel_id=1, source_target_pairs={{0,24},{8,0},{16,8},{24,16},{1,25},{9,1},{17,9},{25,17},{2,26},{10... | collective-permute-start | bytes 147464 | tf_op jit(solution)/shard_map/ppermute | solution.py:360
  762.3 40.5 %collective-permute-start.106 = (bf16[256,1536]{1,0:T(8,128)(2,1)S(1)}, bf16[256,1536]{1,0:T(8,128)(2,1)S(1)}, u32[]{:S(2)}, u32[]{:S(2)}) collective-permute-start(bf16[256,1536]{1,0:T(8,128)(2,1)S(1)} %copy-done.27), channel_id=1, source_target_pairs={{0,4},{4,0},{1,5},{5,1},{2,6},{6,2},{3,7},{7,3},{8,12},{12,8},{9,1... | collective-permute-start | bytes 2359304 | tf_op jit(solution)/shard_map/ppermute | solution.py:345
  765.1 40.7 %collective-permute-start.107 = (bf16[256,1536]{1,0:T(8,128)(2,1)S(1)}, bf16[256,1536]{1,0:T(8,128)(2,1)S(1)}, u32[]{:S(2)}, u32[]{:S(2)}) collective-permute-start(bf16[256,1536]{1,0:T(8,128)(2,1)S(1)} %copy-done.27), channel_id=1, source_target_pairs={{0,2},{2,0},{1,3},{3,1},{4,6},{6,4},{5,7},{7,5},{8,10},{10,8},{9,1... | collective-permute-start | bytes 2359304 | tf_op jit(solution)/shard_map/ppermute | solution.py:345
  765.1 62.0 %collective-permute-start.115 = (bf16[512,1024]{1,0:T(8,128)(2,1)S(1)}, bf16[512,1024]{1,0:T(8,128)(2,1)}, u32[]{:S(2)}, u32[]{:S(2)}) collective-permute-start(bf16[512,1024]{1,0:T(8,128)(2,1)S(1)} %pad_maximum_fusion.19.refs_0_), channel_id=1, source_target_pairs={{0,4},{4,0},{1,5},{5,1},{2,6},{6,2},{3,7},{7,3},{8,12},{12,8},{9,1... | collective-permute-start | bytes 3145736 | tf_op jit(solution)/shard_map/ppermute | solution.py:345
  799.0 29.0 %collective-permute-start.96 = (bf16[128,2560]{1,0:T(8,128)(2,1)S(1)}, bf16[128,2560]{1,0:T(8,128)(2,1)S(1)}, u32[]{:S(2)}, u32[]{:S(2)}) collective-permute-start(bf16[128,2560]{1,0:T(8,128)(2,1)S(1)} %pad_maximum_fusion.24), channel_id=1, source_target_pairs={{0,8},{8,0},{16,24},{24,16},{1,9},{9,1},{17,25},{25,17},{2,10},{10... | collective-permute-start | bytes 1966088 | tf_op jit(solution)/shard_map/ppermute | solution.py:348
  805.8 46.6 %collective-permute-start.126 = (bf16[512,1024]{1,0:T(8,128)(2,1)S(1)}, bf16[512,1024]{1,0:T(8,128)(2,1)S(1)}, u32[]{:S(2)}, u32[]{:S(2)}) collective-permute-start(bf16[512,1024]{1,0:T(8,128)(2,1)S(1)} %collective-permute-done.124.refs_1_), channel_id=1, source_target_pairs={{0,2},{2,0},{1,3},{3,1},{4,6},{6,4},{5,7},{7,5},{8,10},{10,8},{9,1... | collective-permute-start | bytes 3145736 | tf_op jit(solution)/shard_map/ppermute | solution.py:345
  818.1 40.4 %collective-permute-start.116 = (bf16[512,1024]{1,0:T(8,128)(2,1)S(1)}, bf16[512,1024]{1,0:T(8,128)(2,1)S(1)}, u32[]{:S(2)}, u32[]{:S(2)}) collective-permute-start(bf16[512,1024]{1,0:T(8,128)(2,1)S(1)} %pad_maximum_fusion.19.refs_0_), channel_id=1, source_target_pairs={{0,2},{2,0},{1,3},{3,1},{4,6},{6,4},{5,7},{7,5},{8,10},{10,8},{9,1... | collective-permute-start | bytes 3145736 | tf_op jit(solution)/shard_map/ppermute | solution.py:345
  827.1 32.6 %collective-permute-start.108 = (bf16[256,1536]{1,0:T(8,128)(2,1)S(1)}, bf16[256,1536]{1,0:T(8,128)(2,1)S(1)}, u32[]{:S(2)}, u32[]{:S(2)}) collective-permute-start(bf16[256,1536]{1,0:T(8,128)(2,1)S(1)} %collective-permute-done.106.refs_1_), channel_id=1, source_target_pairs={{0,2},{2,0},{1,3},{3,1},{4,6},{6,4},{5,7},{7,5},{8,10},{10,8},{9,1... | collective-permute-start | bytes 2359304 | tf_op jit(solution)/shard_map/ppermute | solution.py:345
  841.8 35.4 %collective-permute-start.97 = (bf16[256,2560]{1,0:T(8,128)(2,1)}, bf16[256,2560]{1,0:T(8,128)(2,1)}, u32[]{:S(2)}, u32[]{:S(2)}) collective-permute-start(bf16[256,2560]{1,0:T(8,128)(2,1)} %pad_maximum_fusion.15.refs_0_), channel_id=1, source_target_pairs={{0,4},{4,0},{1,5},{5,1},{2,6},{6,2},{3,7},{7,3},{8,12},{12,8},{9,1... | collective-permute-start | bytes 3932168 | tf_op jit(solution)/shard_map/ppermute | solution.py:345
  852.4 47.2 %collective-permute-start.88 = (bf16[512,1024]{1,0:T(8,128)(2,1)}, bf16[512,1024]{1,0:T(8,128)(2,1)}, u32[]{:S(2)}, u32[]{:S(2)}) collective-permute-start(bf16[512,1024]{1,0:T(8,128)(2,1)} %pad_maximum_fusion.18.refs_0_), channel_id=1, source_target_pairs={{0,4},{4,0},{1,5},{5,1},{2,6},{6,2},{3,7},{7,3},{8,12},{12,8},{9,1... | collective-permute-start | bytes 3145736 | tf_op jit(solution)/shard_map/ppermute | solution.py:345
  859.4 40.2 %collective-permute-start.89 = (bf16[512,1024]{1,0:T(8,128)(2,1)}, bf16[512,1024]{1,0:T(8,128)(2,1)}, u32[]{:S(2)}, u32[]{:S(2)}) collective-permute-start(bf16[512,1024]{1,0:T(8,128)(2,1)} %pad_maximum_fusion.18.refs_0_), channel_id=1, source_target_pairs={{0,2},{2,0},{1,3},{3,1},{4,6},{6,4},{5,7},{7,5},{8,10},{10,8},{9,1... | collective-permute-start | bytes 3145736 | tf_op jit(solution)/shard_map/ppermute | solution.py:345
  860.6 56.8 %collective-permute-start.79 = (bf16[512,1024]{1,0:T(8,128)(2,1)}, bf16[512,1024]{1,0:T(8,128)(2,1)}, u32[]{:S(2)}, u32[]{:S(2)}) collective-permute-start(bf16[512,1024]{1,0:T(8,128)(2,1)} %pad_maximum_fusion.17.refs_0_), channel_id=1, source_target_pairs={{0,4},{4,0},{1,5},{5,1},{2,6},{6,2},{3,7},{7,3},{8,12},{12,8},{9,1... | collective-permute-start | bytes 3145736 | tf_op jit(solution)/shard_map/ppermute | solution.py:345
  861.5 81.4 %collective-permute-start.98 = (bf16[256,2560]{1,0:T(8,128)(2,1)}, bf16[256,2560]{1,0:T(8,128)(2,1)S(1)}, u32[]{:S(2)}, u32[]{:S(2)}) collective-permute-start(bf16[256,2560]{1,0:T(8,128)(2,1)} %pad_maximum_fusion.15.refs_0_), channel_id=1, source_target_pairs={{0,2},{2,0},{1,3},{3,1},{4,6},{6,4},{5,7},{7,5},{8,10},{10,8},{9,1... | collective-permute-start | bytes 3932168 | tf_op jit(solution)/shard_map/ppermute | solution.py:345
  877.2 65.7 %collective-permute-start.99 = (bf16[256,2560]{1,0:T(8,128)(2,1)}, bf16[256,2560]{1,0:T(8,128)(2,1)S(1)}, u32[]{:S(2)}, u32[]{:S(2)}) collective-permute-start(bf16[256,2560]{1,0:T(8,128)(2,1)} %collective-permute-done.97.refs_1_), channel_id=1, source_target_pairs={{0,2},{2,0},{1,3},{3,1},{4,6},{6,4},{5,7},{7,5},{8,10},{10,8},{9,1... | collective-permute-start | bytes 3932168 | tf_op jit(solution)/shard_map/ppermute | solution.py:345
  899.7 51.8 %collective-permute-start.80 = (bf16[512,1024]{1,0:T(8,128)(2,1)}, bf16[512,1024]{1,0:T(8,128)(2,1)S(1)}, u32[]{:S(2)}, u32[]{:S(2)}) collective-permute-start(bf16[512,1024]{1,0:T(8,128)(2,1)} %pad_maximum_fusion.17.refs_0_), channel_id=1, source_target_pairs={{0,2},{2,0},{1,3},{3,1},{4,6},{6,4},{5,7},{7,5},{8,10},{10,8},{9,1... | collective-permute-start | bytes 3145736 | tf_op jit(solution)/shard_map/ppermute | solution.py:345
  899.7 37.9 %collective-permute-start.90 = (bf16[512,1024]{1,0:T(8,128)(2,1)}, bf16[512,1024]{1,0:T(8,128)(2,1)}, u32[]{:S(2)}, u32[]{:S(2)}) collective-permute-start(bf16[512,1024]{1,0:T(8,128)(2,1)} %collective-permute-done.88.refs_1_), channel_id=1, source_target_pairs={{0,2},{2,0},{1,3},{3,1},{4,6},{6,4},{5,7},{7,5},{8,10},{10,8},{9,1... | collective-permute-start | bytes 3145736 | tf_op jit(solution)/shard_map/ppermute | solution.py:345
  917.4 34.1 %collective-permute-start.81 = (bf16[512,1024]{1,0:T(8,128)(2,1)}, bf16[512,1024]{1,0:T(8,128)(2,1)S(1)}, u32[]{:S(2)}, u32[]{:S(2)}) collective-permute-start(bf16[512,1024]{1,0:T(8,128)(2,1)} %collective-permute-done.79.refs_1_), channel_id=1, source_target_pairs={{0,2},{2,0},{1,3},{3,1},{4,6},{6,4},{5,7},{7,5},{8,10},{10,8},{9,1... | collective-permute-start | bytes 3145736 | tf_op jit(solution)/shard_map/ppermute | solution.py:345
  (185 other events, 2512.3 us)
